TPU v7x, 256 devices: a whole 4x4x8 slice. The times are simulated.
256 devices in a mesh: box: 256 (over z, y, x, core).
Axes of the slice: x: 4, y: 4, z: 8, core: 2. Of those that a mesh axis runs over, the one named last changes fastest.
Arguments:
- fine_mult: bfloat16 [262144, 128], P('box'), may hold values from -6 to 6
- parent_mult: bfloat16 [32768, 128], P('box'), may hold values from -6 to 6
- fine_mask: int32 [20, 262144], P(None, 'box'), may hold values from 0 to 65535, as said below
- parent_mask: int32 [20, 32768], P(None, 'box'), may hold values from 0 to 65535, as said below
- kernels: bfloat16 [316, 128, 128], replicated, may hold values from -0.0390625 to 0.0390625
- shift_ops: bfloat16 [8, 128, 128], replicated, may hold values from -0.5 to 0.5
Outputs:
- fine_local: bfloat16 [262144, 128], P('box')
- parent_local: bfloat16 [32768, 128], P('box')
Inputs may be any that keep to these rules, and one draw needn't show every extreme that they name: `fine_mask`: bit d mod 16 of word floor(d / 16) of box t is set only where the box at t's coordinates plus offset d lies inside the grid and its parent is one of the 27 boxes around t's parent; bits 12 to 15 of word 19 are zero; sources in many regions are missing from the lists. `parent_mask`: the same rule at the parent level.
All inputs are finite; a program needn't handle non-finite values.
Results may differ from a plain program's by a relative error of at most 0.0027.
Values may be sent and summed in bfloat16 or wider, within the bound.
No kernel may reach another device: no remote copies, remote signals or barrier semaphores. Data moves between devices by JAX's collectives and lax.ppermute only.
A program may use at most 320 MiB of HBM per device.

v0:
```python
import jax
import jax.numpy as jnp
import numpy as np
from jax import lax
from jax.experimental import pallas as pl
from jax.experimental.pallas import tpu as pltpu
from jax.sharding import PartitionSpec as P

DIM_OF_BIT = (2, 1, 0)


def direction_table():
    listing = []
    picks = ([-2, -1, 0, 1, 2], [-3], [3])
    for ga in range(3):
        for gb in range(3):
            for gc in range(3):
                for oa in picks[ga]:
                    for ob in picks[gb]:
                        for oc in picks[gc]:
                            if max(abs(oa), abs(ob), abs(oc)) >= 2:
                                listing.append((oa, ob, oc, ga, gb, gc))
    return np.array(listing, np.int32)


def grid_order(total_bits):
    axes_order = []
    extents = []
    for target in range(3):
        chosen = [k for k in range(total_bits - 1, -1, -1) if 2 - k % 3 == target]
        axes_order += [total_bits - 1 - k for k in chosen]
        extents.append(2 ** len(chosen))
    return axes_order, extents


def to_grid(rows, total_bits):
    axes_order, extents = grid_order(total_bits)
    trailing = rows.shape[1:]
    bitwise = rows.reshape((2,) * total_bits + trailing)
    extra = tuple(range(total_bits, total_bits + len(trailing)))
    return jnp.transpose(bitwise, tuple(axes_order) + extra).reshape(tuple(extents) + trailing)


def grid_permutation(total_bits):
    axes_order, _ = grid_order(total_bits)
    numbers = np.arange(2**total_bits).reshape((2,) * total_bits)
    return np.transpose(numbers, axes_order).reshape(-1)


def octant_grids(rows, total_bits):
    width = rows.shape[1]
    parents = to_grid(rows.reshape(-1, 8, width), total_bits - 3)
    return jnp.moveaxis(parents, 3, 0)


def owned_bits(dim, low_bits, device_bits):
    return [k for k in range(device_bits) if 2 - (low_bits + k) % 3 == dim]


def pair_route(dim, odd, low_bits, device_bits):
    bits = owned_bits(dim, low_bits, device_bits)
    route = []
    for number in range(2**device_bits):
        place = sum(((number >> bit) & 1) << k for k, bit in enumerate(bits))
        other = place + (1 if place % 2 == odd else -1)
        if 0 <= other < 2 ** len(bits):
            target = number
            for k, bit in enumerate(bits):
                target = target & ~(1 << bit) | ((other >> k) & 1) << bit
            route.append((number, target))
    return route


def exchange(fine, parent, dim, low_bits, device_index, device_bits):
    first_bit = owned_bits(dim, low_bits, device_bits)[0]
    is_odd = (jnp.right_shift(device_index, first_bit) & 1) == 1
    axis = dim + 1

    def face(block, last):
        at = block.shape[axis] - 1 if last else 0
        return lax.index_in_dim(block, at, axis, keepdims=False)

    def packed(last):
        pieces = [face(b, last).reshape(8, -1, b.shape[-1]) for b in (fine, parent)]
        return jnp.concatenate(pieces, axis=1)

    top = packed(True)
    bottom = packed(False)
    even_send = jnp.where(is_odd, bottom, top)
    odd_send = jnp.where(is_odd, top, bottom)
    odd_got = lax.ppermute(odd_send, "box", pair_route(dim, 1, low_bits, device_bits))
    even_got = lax.ppermute(even_send, "box", pair_route(dim, 0, low_bits, device_bits))
    below = jnp.where(is_odd, even_got, odd_got)
    above = jnp.where(is_odd, odd_got, even_got)
    split = face(fine, True).size // (8 * fine.shape[-1])
    out = []
    for block, pick in ((fine, slice(0, split)), (parent, slice(split, None))):
        shape = face(block, True).shape
        low = jnp.expand_dims(below[:, pick].reshape(shape), axis)
        high = jnp.expand_dims(above[:, pick].reshape(shape), axis)
        out.append(jnp.concatenate([low, block, high], axis=axis))
    return out


def tables(fine_rows, slab_rows):
    offsets = direction_table()
    count = offsets.shape[0]
    fine_at = np.zeros((8, count), np.int32)
    parent_at = np.zeros((8, count), np.int32)
    for octant in range(8):
        parity = np.array([octant >> 2 & 1, octant >> 1 & 1, octant & 1])
        moved = offsets[:, :3] + parity
        source = moved & 1
        shift = np.clip((moved >> 1) + 1, 0, 2)
        source_octant = source[:, 0] * 4 + source[:, 1] * 2 + source[:, 2]
        fine_at[octant] = (
            (shift[:, 1] * 3 + shift[:, 2]) * 8 + source_octant
        ) * fine_rows + shift[:, 0] * slab_rows
        parent_at[octant] = (
            (shift[:, 0] * 3 + shift[:, 1]) * 3 + shift[:, 2]
        ) * 8 + source_octant
    return fine_at, parent_at


def group_lists():
    offsets = direction_table()
    runs = []
    start = 0
    for number in range(1, offsets.shape[0] + 1):
        if number == offsets.shape[0] or tuple(offsets[number, 3:]) != tuple(offsets[start, 3:]):
            markers = [int(v) for v in offsets[start, 3:]]
            octants = []
            for octant in range(8):
                parity = (octant >> 2 & 1, octant >> 1 & 1, octant & 1)
                if all(m == 0 or (m == 1 and p == 1) or (m == 2 and p == 0) for m, p in zip(markers, parity)):
                    octants.append(octant)
            runs.append((start, number, octants))
            start = number
    return runs


def make_kernel(F, G, words, classes, copies):
    rows = F + G

    def kernel(fine_at, parent_at, starts, octs, masks, x, xp, kern, shift, perm, fine_out,
               parent_out, wbuf, mbuf, lhs, acc, sems):
        loads = []
        for number, (lo, hi) in enumerate(copies):
            cp = pltpu.make_async_copy(kern.at[pl.ds(lo * 128, (hi - lo) * 128)],
                                       wbuf.at[pl.ds(lo * 128, (hi - lo) * 128)], sems.at[number])
            cp.start()
            loads.append(cp)

        def spread(p, carry):
            for w in range(words):
                column = masks[p, :, w : w + 1]
                mbuf[w, p] = jnp.broadcast_to(column, (rows, 128)).astype(jnp.int16)
            return carry

        lax.fori_loop(0, 8, spread, 0)
        acc[...] = jnp.zeros_like(acc)

        def fill(slot, octant, d, column):
            word = d // 16
            bit = jnp.left_shift(1, d % 16)
            wanted = jnp.broadcast_to(bit, (16, 128)).astype(jnp.int16)
            zero = jnp.zeros((16, 128), jnp.bfloat16)
            none = jnp.zeros((16, 128), jnp.int16)
            at_f = pl.multiple_of(fine_at[octant, d], 16)
            at_p = parent_at[octant, d]
            for r in range(rows // 16):
                held = mbuf[word, octant, r * 16 : r * 16 + 16, :]
                if r * 16 < F:
                    value = x[pl.ds(pl.multiple_of(at_f + r * 16, 16), 16), :]
                else:
                    value = xp[at_p]
                kept = jnp.where((held & wanted) != none, value, zero)
                lhs[slot * rows + r * 16 : slot * rows + r * 16 + 16, column * 128 : column * 128 + 128] = kept

        def run_class(first_table, chunk, lanes):
            def step(number, carry):
                d0 = starts[number]
                for j in range(chunk):
                    for i in range(lanes):
                        octant = i if lanes == 8 else octs[number, i]
                        fill(i, octant, d0 + j, j)
                weights = wbuf[pl.ds(pl.multiple_of(d0 * 128, 128), chunk * 128), :]
                got = jnp.dot(lhs[: lanes * rows, : chunk * 128], weights, preferred_element_type=jnp.float32)
                for i in range(lanes):
                    octant = i if lanes == 8 else octs[number, i]
                    acc[octant] += got[i * rows : (i + 1) * rows]
                return carry

            return step

        done = 0
        for lanes, chunk, first, last, ready in classes:
            while done < ready:
                loads[done].wait()
                done += 1
            lax.fori_loop(first, last, run_class(first, chunk, lanes), 0)

        far = []
        for p in range(8):
            far.append((acc[p, F:, :] * 0.5).astype(jnp.bfloat16))
        local = jnp.concatenate(far, axis=0)
        parent_out[...] = local
        ordered = jnp.dot(perm[...], local, preferred_element_type=jnp.float32).astype(jnp.bfloat16)
        for p in range(8):
            moved = jnp.dot(ordered, shift[p], preferred_element_type=jnp.float32)
            fine_out[p] = (acc[p, :F, :] + moved).astype(jnp.bfloat16)

    return kernel


def on_device(fine_mult, parent_mult, fine_mask, parent_mask, kernels, shift_ops):
    device_bits = lax.axis_size("box").bit_length() - 1
    device_index = lax.axis_index("box")
    fine_bits = fine_mult.shape[0].bit_length() - 1
    parent_bits = parent_mult.shape[0].bit_length() - 1
    width = fine_mult.shape[1]
    count = kernels.shape[0]
    words = fine_mask.shape[0]
    fine = octant_grids(fine_mult, fine_bits)
    parent = octant_grids(parent_mult, parent_bits)
    F = fine_mult.shape[0] // 8
    G = parent_mult.shape[0] // 8
    n1, n2, n3 = fine.shape[1:4]
    m1, m2, m3 = parent.shape[1:4]
    masks = jnp.concatenate(
        [
            octant_grids(fine_mask.T, fine_bits).reshape(8, F, words),
            octant_grids(parent_mask.T, parent_bits).reshape(8, G, words),
        ],
        axis=1,
    )
    for dim in (1, 2, 0):
        fine, parent = exchange(fine, parent, dim, fine_bits, device_index, device_bits)
    x = jnp.stack(
        [
            fine[:, :, b : b + n2, c : c + n3].reshape(8, -1, width)
            for b in range(3)
            for c in range(3)
        ]
    ).reshape(-1, width)
    xp = jnp.stack(
        [
            parent[:, a : a + m1, b : b + m2, c : c + m3].reshape(8, G, width)
            for a in range(3)
            for b in range(3)
            for c in range(3)
        ]
    ).reshape(-1, G, width)
    fine_at, parent_at = tables((n1 + 2) * n2 * n3, n2 * n3)
    runs = group_lists()
    starts = []
    octs = []
    classes = []
    bounds = [0, 98, 173, 248, count]
    copies = list(zip(bounds[:-1], bounds[1:]))
    for lanes, chunk in ((8, 7), (4, 5), (2, 5), (1, 1)):
        first = len(starts)
        for lo, hi, octants in runs:
            if len(octants) == lanes:
                for at in range(lo, hi, chunk):
                    starts.append(at)
                    octs.append((octants + [0] * 8)[:8])
        classes.append((lanes, chunk, first, len(starts), 1 if lanes == 8 else len(copies)))
    parent_numbers = np.arange(parent_mult.shape[0]).reshape(-1, 8)
    order_pg = grid_permutation(parent_bits - 3)
    held = parent_numbers[order_pg].T.reshape(-1)
    wanted = grid_permutation(parent_bits)
    place = np.zeros(parent_mult.shape[0], np.int64)
    place[held] = np.arange(parent_mult.shape[0])
    perm = np.zeros((F, F), np.float32)
    perm[np.arange(F), place[wanted]] = 1
    rows = F + G
    vmem = pl.BlockSpec(memory_space=pltpu.VMEM)
    smem = pl.BlockSpec(memory_space=pltpu.SMEM)
    fine_local, parent_local = pl.pallas_call(
        make_kernel(F, G, words, classes, copies),
        out_shape=(
            jax.ShapeDtypeStruct((8, F, width), jnp.bfloat16),
            jax.ShapeDtypeStruct((8 * G, width), jnp.bfloat16),
        ),
        in_specs=[smem, smem, smem, smem, vmem, vmem, vmem, pl.BlockSpec(memory_space=pl.ANY), vmem, vmem],
        out_specs=(vmem, vmem),
        scratch_shapes=[
            pltpu.VMEM((count * width, width), jnp.bfloat16),
            pltpu.VMEM((words, 8, rows, 128), jnp.int16),
            pltpu.VMEM((8 * rows, 7 * width), jnp.bfloat16),
            pltpu.VMEM((8, rows, width), jnp.float32),
            pltpu.SemaphoreType.DMA((len(copies),)),
        ],
        compiler_params=pltpu.CompilerParams(vmem_limit_bytes=48 << 20),
        name="translate",
    )(
        jnp.asarray(fine_at),
        jnp.asarray(parent_at),
        jnp.asarray(np.array(starts, np.int32)),
        jnp.asarray(np.array(octs, np.int32)),
        masks,
        x,
        xp,
        kernels.reshape(-1, width),
        shift_ops,
        jnp.asarray(perm, jnp.bfloat16),
    )
    back_f = np.argsort(grid_permutation(fine_bits - 3))
    back_g = np.argsort(grid_permutation(parent_bits - 3))
    del back_f, back_g
    fine_local = from_octants(fine_local, fine_bits)
    parent_local = from_octants(parent_local.reshape(8, G, width), parent_bits)
    return fine_local, parent_local


def from_octants(blocks, total_bits):
    width = blocks.shape[-1]
    axes_order, extents = grid_order(total_bits - 3)
    bits = total_bits - 3
    grid = blocks.reshape((8,) + (2,) * bits + (width,))
    inverse = [0] * bits
    for position, source in enumerate(axes_order):
        inverse[source] = position
    moved = jnp.transpose(grid, tuple(1 + v for v in inverse) + (0, bits + 1))
    return moved.reshape(2**total_bits, width)


def solution(mesh):
    return jax.shard_map(
        on_device,
        mesh=mesh,
        in_specs=(P("box", None), P("box", None), P(None, "box"), P(None, "box"), P(), P()),
        out_specs=(P("box", None), P("box", None)),
        check_vma=False,
    )
```

profile of v0, /device:TPU:169, one launch (start us, length us, event | category | flops | bytes accessed | tf_op | source)
XLA Modules:
  0.0 92.9 jit_solution(9553402183812402676)
XLA Ops:
  0.6 0.8 copy.175
  1.4 1.0 %copy.174 = bf16[2,2,2,2,2,2,2,8,128]{8,7,6,5,4,3,2,1,0:T(8,128)(2,1)S(1)} copy(bf16[2,2,2,2,2,2,2,8,128]{8,7,6,3,1,5,2,0,4:T(8,128)(2,1)} %bitcast.169) | data formatting | bytes 524288 | tf_op jit(solution)/shard_map/transpose | solution.py:41
  2.4 0.8 collective-permute-start
  3.2 2.9 %collective-permute-start.1 = (bf16[8,40,128]{2,0,1:T(8,128)(2,1)S(1)}, bf16[8,40,128]{2,0,1:T(8,128)(2,1)S(1)}, u32[]{:S(2)}, u32[]{:S(2)}) collective-permute-start(bf16[8,40,128]{2,0,1:T(8,128)(2,1)S(1)} %get-tuple-element.28), channel_id=1, source_target_pairs={{1,8},{3,10},{5,12},{7,14},{8,1},{9,64},{10,3},{11,66},{12,5},{13,... | collective-permute-start | bytes 245768 | tf_op jit(solution)/shard_map/ppermute | solution.py:91
  6.1 1.1 %copy.168 = s32[20,1024]{0,1:T(8,128)S(1)} copy(s32[20,1024]{1,0:T(8,128)} %param.13) | data formatting | bytes 163840 | tf_op args[2]
  7.2 0.1 copy.169
  7.3 0.1 copy.170
  7.4 0.1 copy.171
  7.6 3.2 %collective-permute-done.1 = bf16[8,40,128]{2,0,1:T(8,128)(2,1)S(1)} collective-permute-done((bf16[8,40,128]{2,0,1:T(8,128)(2,1)S(1)}, bf16[8,40,128]{2,0,1:T(8,128)(2,1)S(1)}, u32[]{:S(2)}, u32[]{:S(2)}) %collective-permute-start.1) | collective-permute-done | bytes 81952 | tf_op jit(solution)/shard_map/ppermute | solution.py:91
  11.0 2.8 %collective-permute-start.2 = (bf16[8,32,128]{2,0,1:T(8,128)(2,1)S(1)}, bf16[8,32,128]{2,0,1:T(8,128)(2,1)S(1)}, u32[]{:S(2)}, u32[]{:S(2)}) collective-permute-start(bf16[8,32,128]{2,0,1:T(8,128)(2,1)S(1)} %get-tuple-element.49), channel_id=1, source_target_pairs={{0,4},{1,5},{2,6},{3,7},{4,0},{5,1},{6,2},{7,3},{8,12},{9,13},{10,... | collective-permute-start | bytes 196616 | tf_op jit(solution)/shard_map/ppermute | solution.py:92
  13.8 3.3 %collective-permute-start.3 = (bf16[8,32,128]{2,0,1:T(8,128)(2,1)S(1)}, bf16[8,32,128]{2,0,1:T(8,128)(2,1)S(1)}, u32[]{:S(2)}, u32[]{:S(2)}) collective-permute-start(bf16[8,32,128]{2,0,1:T(8,128)(2,1)S(1)} %get-tuple-element.50), channel_id=1, source_target_pairs={{4,32},{5,33},{6,34},{7,35},{12,40},{13,41},{14,42},{15,43},{20,48... | collective-permute-start | bytes 196616 | tf_op jit(solution)/shard_map/ppermute | solution.py:91
  17.2 4.1 %collective-permute-done.3 = bf16[8,32,128]{2,0,1:T(8,128)(2,1)S(1)} collective-permute-done((bf16[8,32,128]{2,0,1:T(8,128)(2,1)S(1)}, bf16[8,32,128]{2,0,1:T(8,128)(2,1)S(1)}, u32[]{:S(2)}, u32[]{:S(2)}) %collective-permute-start.3) | collective-permute-done | bytes 65568 | tf_op jit(solution)/shard_map/ppermute | solution.py:91
  21.5 0.1 pad_maximum_fusion.8
  21.6 0.3 collective-permute-start.4
  21.9 3.8 %collective-permute-start.5 = (bf16[8,84,128]{2,0,1:T(8,128)(2,1)S(1)}, bf16[8,84,128]{2,0,1:T(8,128)(2,1)S(1)}, u32[]{:S(2)}, u32[]{:S(2)}) collective-permute-start(bf16[8,84,128]{2,0,1:T(8,128)(2,1)S(1)} %get-tuple-element.22), channel_id=1, source_target_pairs={{2,16},{3,17},{6,20},{7,21},{10,24},{11,25},{14,28},{15,29},{16,2}... | collective-permute-start | bytes 516104 | tf_op jit(solution)/shard_map/ppermute | solution.py:91
  25.8 2.1 %collective-permute-done.4 = bf16[8,84,128]{2,0,1:T(8,128)(2,1)S(1)} collective-permute-done((bf16[8,84,128]{2,0,1:T(8,128)(2,1)S(1)}, bf16[8,84,128]{2,0,1:T(8,128)(2,1)S(1)}, u32[]{:S(2)}, u32[]{:S(2)}) %collective-permute-start.4) | collective-permute-done | bytes 172064 | tf_op jit(solution)/shard_map/ppermute | solution.py:92
  27.9 11.1 %collective-permute-done.5 = bf16[8,84,128]{2,0,1:T(8,128)(2,1)S(1)} collective-permute-done((bf16[8,84,128]{2,0,1:T(8,128)(2,1)S(1)}, bf16[8,84,128]{2,0,1:T(8,128)(2,1)S(1)}, u32[]{:S(2)}, u32[]{:S(2)}) %collective-permute-start.5) | collective-permute-done | bytes 172064 | tf_op jit(solution)/shard_map/ppermute | solution.py:91
  39.2 0.1 fusion.2
  39.3 0.2 pad_maximum_fusion
  39.4 0.7 fusion
  40.1 0.1 copy_dynamic-update-slice_fusion.8
  40.7 0.1 copy_dynamic-update-slice_fusion.7
  40.8 0.1 copy_dynamic-update-slice_fusion.6
  40.9 0.1 copy_dynamic-update-slice_fusion.5
  41.0 0.1 copy_dynamic-update-slice_fusion.4
  41.1 0.1 copy_dynamic-update-slice_fusion.3
  41.2 0.1 copy_dynamic-update-slice_fusion.2
  41.3 0.1 copy_dynamic-update-slice_fusion.1
  41.4 0.1 copy_dynamic-update-slice_fusion
  41.6 49.7 %translate.1 = (bf16[8,128,128]{2,1,0:T(8,128)(2,1)S(1)}, bf16[128,128]{1,0:T(8,128)(2,1)S(1)}) custom-call(s32[8,316]{1,0:T(8,128)S(1)} %copy-done.3, s32[8,316]{1,0:T(8,128)S(1)} %copy-done.4, s32[64]{0:T(128)S(1)} %copy-done.5, s32[64,8]{1,0:T(8,128)S(1)} %copy-done.1, s32[8,144,20]{2,1,0:T(8,128)S(1)} %pad_add_fusion.masks, ...), custom_call_target="tpu_custom_call" | custom-call | tf_op jit(solution)/shard_map/translate/pallas_call | solution.py:280
  91.3 1.0 %copy.218 = bf16[2,2,2,2,2,2,2,8,128]{8,7,6,5,4,3,2,1,0:T(8,128)(2,1)} copy(bf16[2,2,2,2,2,2,2,8,128]{8,6,3,0,5,2,4,1,7:T(2,128)(2,1)S(1)} %bitcast.112) | data formatting | bytes 524288 | tf_op jit(solution)/shard_map/transpose | solution.py:325
  92.3 0.6 copy.219
  (74 shorter events, 0.9 us)
Async XLA Ops:
  0.6 6.8 %copy-start.6 = (s32[20,128]{1,0:T(8,128)S(1)}, s32[20,128]{1,0:T(8,128)}, u32[]{:S(2)}) copy-start(s32[20,128]{1,0:T(8,128)} %param.14) | copy-start | bytes 30724
  2.4 5.2 %collective-permute-start = (bf16[8,40,128]{2,0,1:T(8,128)(2,1)S(1)}, bf16[8,40,128]{2,0,1:T(8,128)(2,1)S(1)}, u32[]{:S(2)}, u32[]{:S(2)}) collective-permute-start(bf16[8,40,128]{2,0,1:T(8,128)(2,1)S(1)} %get-tuple-element.27), channel_id=1, source_target_pairs={{0,1},{1,0},{2,3},{3,2},{4,5},{5,4},{6,7},{7,6},{8,9},{9,8},{10,11... | collective-permute-start | bytes 245768 | tf_op jit(solution)/shard_map/ppermute | solution.py:92
  3.2 7.6 %collective-permute-start.1 = (bf16[8,40,128]{2,0,1:T(8,128)(2,1)S(1)}, bf16[8,40,128]{2,0,1:T(8,128)(2,1)S(1)}, u32[]{:S(2)}, u32[]{:S(2)}) collective-permute-start(bf16[8,40,128]{2,0,1:T(8,128)(2,1)S(1)} %get-tuple-element.28), channel_id=1, source_target_pairs={{1,8},{3,10},{5,12},{7,14},{8,1},{9,64},{10,3},{11,66},{12,5},{13,... | collective-permute-start | bytes 245768 | tf_op jit(solution)/shard_map/ppermute | solution.py:91
  11.0 6.2 %collective-permute-start.2 = (bf16[8,32,128]{2,0,1:T(8,128)(2,1)S(1)}, bf16[8,32,128]{2,0,1:T(8,128)(2,1)S(1)}, u32[]{:S(2)}, u32[]{:S(2)}) collective-permute-start(bf16[8,32,128]{2,0,1:T(8,128)(2,1)S(1)} %get-tuple-element.49), channel_id=1, source_target_pairs={{0,4},{1,5},{2,6},{3,7},{4,0},{5,1},{6,2},{7,3},{8,12},{9,13},{10,... | collective-permute-start | bytes 196616 | tf_op jit(solution)/shard_map/ppermute | solution.py:92
  13.8 7.5 %collective-permute-start.3 = (bf16[8,32,128]{2,0,1:T(8,128)(2,1)S(1)}, bf16[8,32,128]{2,0,1:T(8,128)(2,1)S(1)}, u32[]{:S(2)}, u32[]{:S(2)}) collective-permute-start(bf16[8,32,128]{2,0,1:T(8,128)(2,1)S(1)} %get-tuple-element.50), channel_id=1, source_target_pairs={{4,32},{5,33},{6,34},{7,35},{12,40},{13,41},{14,42},{15,43},{20,48... | collective-permute-start | bytes 196616 | tf_op jit(solution)/shard_map/ppermute | solution.py:91
  21.6 6.3 %collective-permute-start.4 = (bf16[8,84,128]{2,0,1:T(8,128)(2,1)S(1)}, bf16[8,84,128]{2,0,1:T(8,128)(2,1)S(1)}, u32[]{:S(2)}, u32[]{:S(2)}) collective-permute-start(bf16[8,84,128]{2,0,1:T(8,128)(2,1)S(1)} %get-tuple-element.21), channel_id=1, source_target_pairs={{0,2},{1,3},{2,0},{3,1},{4,6},{5,7},{6,4},{7,5},{8,10},{9,11},{10,... | collective-permute-start | bytes 516104 | tf_op jit(solution)/shard_map/ppermute | solution.py:92
  21.9 17.1 %collective-permute-start.5 = (bf16[8,84,128]{2,0,1:T(8,128)(2,1)S(1)}, bf16[8,84,128]{2,0,1:T(8,128)(2,1)S(1)}, u32[]{:S(2)}, u32[]{:S(2)}) collective-permute-start(bf16[8,84,128]{2,0,1:T(8,128)(2,1)S(1)} %get-tuple-element.22), channel_id=1, source_target_pairs={{2,16},{3,17},{6,20},{7,21},{10,24},{11,25},{14,28},{15,29},{16,2}... | collective-permute-start | bytes 516104 | tf_op jit(solution)/shard_map/ppermute | solution.py:91
  40.5 1.0 %copy-start = (bf16[8,128,128]{2,1,0:T(8,128)(2,1)S(1)}, bf16[8,128,128]{2,1,0:T(8,128)(2,1)}, u32[]{:S(2)}) copy-start(bf16[8,128,128]{2,1,0:T(8,128)(2,1)} %shift.1) | copy-start | bytes 786436
  40.5 1.0 %copy-start.1 = (s32[64,8]{1,0:T(8,128)S(1)}, s32[64,8]{1,0:T(8,128)}, u32[]{:S(2)}) copy-start(s32[64,8]{1,0:T(8,128)} %constant.23.clone.octs) | copy-start | bytes 6148
  40.5 1.0 %copy-start.2 = (bf16[128,128]{1,0:T(8,128)(2,1)S(1)}, bf16[128,128]{1,0:T(8,128)(2,1)}, u32[]{:S(2)}) copy-start(bf16[128,128]{1,0:T(8,128)(2,1)} %constant.24.clone.perm) | copy-start | bytes 98308
  40.5 1.0 %copy-start.3 = (s32[8,316]{1,0:T(8,128)S(1)}, s32[8,316]{1,0:T(8,128)}, u32[]{:S(2)}) copy-start(s32[8,316]{1,0:T(8,128)} %constant.20.clone.fine_at) | copy-start | bytes 30340
  40.5 1.0 %copy-start.4 = (s32[8,316]{1,0:T(8,128)S(1)}, s32[8,316]{1,0:T(8,128)}, u32[]{:S(2)}) copy-start(s32[8,316]{1,0:T(8,128)} %constant.21.clone.parent_at) | copy-start | bytes 30340
  40.5 1.0 %copy-start.5 = (s32[64]{0:T(128)S(1)}, s32[64]{0:T(128)}, u32[]{:S(2)}) copy-start(s32[64]{0:T(128)} %constant.22.clone.starts) | copy-start | bytes 772
where the time goes:
time: 93.2 us; the launch traced here: 92.9 us
  Pallas kernels  49.7 us (53%)
  waiting for transfers between devices  20.6 us (22%)
  starting transfers between devices  14 us (15%)
  local copies, waits for them, and re-layouts  6.82 us (7%)
  between operations  1.26 us (1%)
    pallas_call x1, Pallas kernels, on_device(): pl.pallas_call(make_kernel(F, G, words, classes, copies), out_shape=(jax....  49.7 us
    ppermute x3, waiting for transfers between devices, exchange(): lax.ppermute(odd_send, 'box', pair_route(dim, 1, low_bits, device_bits))  18.5 us
    ppermute x3, starting transfers between devices, exchange(): lax.ppermute(odd_send, 'box', pair_route(dim, 1, low_bits, device_bits))  10 us
    ppermute x3, starting transfers between devices, exchange(): lax.ppermute(even_send, 'box', pair_route(dim, 0, low_bits, device_bits))  3.94 us
    unnamed x50, local copies, waits for them, and re-layouts  2.3 us
    ppermute x3, waiting for transfers between devices, exchange(): lax.ppermute(even_send, 'box', pair_route(dim, 0, low_bits, device_bits))  2.1 us
  transfers between devices with their start and end apart: 6, of which 4 were waited for; matrix products, arithmetic and copies ran while one was open for 2% of the time, Pallas kernels for 0%

commit v1 on v0

v1 whole, which is shorter than its diff:
```python
import jax
import jax.numpy as jnp
import numpy as np
from jax import lax
from jax.experimental import pallas as pl
from jax.experimental.pallas import tpu as pltpu
from jax.sharding import PartitionSpec as P

DIM_OF_BIT = (2, 1, 0)


def direction_table():
    listing = []
    picks = ([-2, -1, 0, 1, 2], [-3], [3])
    for ga in range(3):
        for gb in range(3):
            for gc in range(3):
                for oa in picks[ga]:
                    for ob in picks[gb]:
                        for oc in picks[gc]:
                            if max(abs(oa), abs(ob), abs(oc)) >= 2:
                                listing.append((oa, ob, oc, ga, gb, gc))
    return np.array(listing, np.int32)


def grid_order(total_bits):
    axes_order = []
    extents = []
    for target in range(3):
        chosen = [k for k in range(total_bits - 1, -1, -1) if 2 - k % 3 == target]
        axes_order += [total_bits - 1 - k for k in chosen]
        extents.append(2 ** len(chosen))
    return axes_order, extents


def to_grid(rows, total_bits):
    axes_order, extents = grid_order(total_bits)
    trailing = rows.shape[1:]
    bitwise = rows.reshape((2,) * total_bits + trailing)
    extra = tuple(range(total_bits, total_bits + len(trailing)))
    return jnp.transpose(bitwise, tuple(axes_order) + extra).reshape(tuple(extents) + trailing)


def grid_permutation(total_bits):
    axes_order, _ = grid_order(total_bits)
    numbers = np.arange(2**total_bits).reshape((2,) * total_bits)
    return np.transpose(numbers, axes_order).reshape(-1)


def octant_grids(rows, total_bits):
    width = rows.shape[1]
    parents = to_grid(rows.reshape(-1, 8, width), total_bits - 3)
    return jnp.moveaxis(parents, 3, 0)


def owned_bits(dim, low_bits, device_bits):
    return [k for k in range(device_bits) if 2 - (low_bits + k) % 3 == dim]


def pair_route(dim, odd, low_bits, device_bits):
    bits = owned_bits(dim, low_bits, device_bits)
    route = []
    for number in range(2**device_bits):
        place = sum(((number >> bit) & 1) << k for k, bit in enumerate(bits))
        other = place + (1 if place % 2 == odd else -1)
        if 0 <= other < 2 ** len(bits):
            target = number
            for k, bit in enumerate(bits):
                target = target & ~(1 << bit) | ((other >> k) & 1) << bit
            route.append((number, target))
    return route


def face(block, axis, last):
    at = block.shape[axis] - 1 if last else 0
    return lax.index_in_dim(block, at, axis, keepdims=False)


def packed_face(fine, parent, axis, last):
    pieces = [face(b, axis, last).reshape(8, -1, b.shape[-1]) for b in (fine, parent)]
    return jnp.concatenate(pieces, axis=1)


def parity(dim, low_bits, device_index, device_bits):
    first_bit = owned_bits(dim, low_bits, device_bits)[0]
    return (jnp.right_shift(device_index, first_bit) & 1) == 1


def exchange(fine, parent, dim, low_bits, device_index, device_bits):
    is_odd = parity(dim, low_bits, device_index, device_bits)
    axis = dim + 1
    top = packed_face(fine, parent, axis, True)
    bottom = packed_face(fine, parent, axis, False)
    even_send = jnp.where(is_odd, bottom, top)
    odd_send = jnp.where(is_odd, top, bottom)
    odd_got = lax.ppermute(odd_send, "box", pair_route(dim, 1, low_bits, device_bits))
    even_got = lax.ppermute(even_send, "box", pair_route(dim, 0, low_bits, device_bits))
    below = jnp.where(is_odd, even_got, odd_got)
    above = jnp.where(is_odd, odd_got, even_got)
    split = face(fine, axis, True).size // (8 * fine.shape[-1])
    out = []
    for block, pick in ((fine, slice(0, split)), (parent, slice(split, None))):
        shape = face(block, axis, True).shape
        low = jnp.expand_dims(below[:, pick].reshape(shape), axis)
        high = jnp.expand_dims(above[:, pick].reshape(shape), axis)
        out.append(jnp.concatenate([low, block, high], axis=axis))
    return out


def odd_groups(dim, low_bits, device_bits):
    paired = pair_route(dim, 1, low_bits, device_bits)
    groups = [[a, b] for a, b in paired if a < b]
    seen = {a for a, _ in paired}
    rest = [number for number in range(2**device_bits) if number not in seen]
    return groups + [[rest[k], rest[k + 1]] for k in range(0, len(rest), 2)]


def shift_lists():
    offsets = direction_table()
    lists = [[[] for _ in range(8)] for _ in range(3)]
    for octant in range(8):
        own = np.array([octant >> 2 & 1, octant >> 1 & 1, octant & 1])
        for number in range(offsets.shape[0]):
            moved = offsets[number, :3] + own
            if moved.min() < -2 or moved.max() > 3:
                continue
            shift = (moved >> 1) + 1
            source = moved & 1
            lists[shift[0]][octant].append((number, shift, source[0] * 4 + source[1] * 2 + source[2]))
    return lists


CHUNK = 18


def work_table(groups, slots, slab_count, slab_rows):
    table = np.zeros((5, 8, slots), np.int32)
    for octant in range(8):
        at = 0
        for place, per_octant in enumerate(groups):
            for number, shift, source in per_octant[octant]:
                across = shift[1] * 3 + shift[2]
                table[0, octant, at] = number
                table[1, octant, at] = (across * 8 + source) * slab_count * slab_rows + shift[0] * slab_rows
                table[2, octant, at] = (place * 9 + across) * 8 + source
                table[3, octant, at] = number // 16
                table[4, octant, at] = 1 << (number % 16)
                at += 1
    return table.reshape(5, 8 * slots)


def spread_masks(masks):
    rows, words = masks.shape[1:]

    def kernel(packed, out):
        def one(octant, carry):
            for w in range(words):
                column = packed[octant, :, w : w + 1]
                out[w, octant] = jnp.broadcast_to(column, (rows, 128)).astype(jnp.int16)
            return carry

        lax.fori_loop(0, 8, one, 0)

    vmem = pl.BlockSpec(memory_space=pltpu.VMEM)
    return pl.pallas_call(
        kernel,
        out_shape=jax.ShapeDtypeStruct((words, 8, rows, 128), jnp.int16),
        in_specs=[vmem],
        out_specs=vmem,
        compiler_params=pltpu.CompilerParams(vmem_limit_bytes=16 << 20),
        name="spread",
    )(masks)


def add_terms(table, slots, words, x, xp, kernels, acc):
    F = acc.shape[1] - xp.shape[1]
    rows = acc.shape[1]

    def masked(octant, at):
        place = octant * slots + at
        wanted = jnp.broadcast_to(table[4, place], (16, 128)).astype(jnp.int16)
        wanted = jnp.broadcast_to(wanted[:1], (rows, 128))
        row = pl.multiple_of(table[1, place], 16)
        value = jnp.concatenate([x[pl.ds(row, F), :], xp[table[2, place]]], axis=0)
        held = words[table[3, place], octant]
        return jnp.where((held & wanted) != 0, value, jnp.zeros_like(value))

    def step(number, carry):
        at = number * CHUNK
        for octant in range(8):
            left = jnp.concatenate([masked(octant, at + j) for j in range(CHUNK)], axis=1)
            right = jnp.concatenate([kernels[table[0, octant * slots + at + j]] for j in range(CHUNK)], axis=0)
            acc[octant] += jnp.dot(left, right, preferred_element_type=jnp.float32)
        return carry

    lax.fori_loop(0, slots // CHUNK, step, 0)


def first_terms(table, slots, words, x, xp, kernels):
    rows = words.shape[2]
    width = kernels.shape[1]

    def kernel(table, words, x, xp, kernels, acc):
        acc[...] = jnp.zeros_like(acc)
        add_terms(table, slots, words, x, xp, kernels, acc)

    vmem = pl.BlockSpec(memory_space=pltpu.VMEM)
    return pl.pallas_call(
        kernel,
        out_shape=jax.ShapeDtypeStruct((8, rows, width), jnp.float32),
        in_specs=[pl.BlockSpec(memory_space=pltpu.SMEM)] + [vmem] * 4,
        out_specs=vmem,
        compiler_params=pltpu.CompilerParams(vmem_limit_bytes=16 << 20),
        name="first_terms",
    )(table, words, x, xp, kernels)


def last_terms(table, slots, words, x, xp, kernels, sums, shift_ops, perm):
    rows = words.shape[2]
    width = kernels.shape[1]
    F = perm.shape[0]

    def kernel(table, words, x, xp, kernels, sums, shift, perm, fine_out, parent_out, acc):
        acc[...] = sums[...]
        add_terms(table, slots, words, x, xp, kernels, acc)
        far = [(acc[p, F:, :] * 0.5).astype(jnp.bfloat16) for p in range(8)]
        local = jnp.concatenate(far, axis=0)
        parent_out[...] = local
        ordered = jnp.dot(perm[...], local, preferred_element_type=jnp.float32).astype(jnp.bfloat16)
        for p in range(8):
            moved = jnp.dot(ordered, shift[p], preferred_element_type=jnp.float32)
            fine_out[p] = (acc[p, :F, :] + moved).astype(jnp.bfloat16)

    vmem = pl.BlockSpec(memory_space=pltpu.VMEM)
    return pl.pallas_call(
        kernel,
        out_shape=(
            jax.ShapeDtypeStruct((8, F, width), jnp.bfloat16),
            jax.ShapeDtypeStruct((8 * (rows - F), width), jnp.bfloat16),
        ),
        in_specs=[pl.BlockSpec(memory_space=pltpu.SMEM)] + [vmem] * 7,
        out_specs=(vmem, vmem),
        scratch_shapes=[pltpu.VMEM((8, rows, width), jnp.float32)],
        compiler_params=pltpu.CompilerParams(vmem_limit_bytes=16 << 20),
        name="last_terms",
    )(table, words, x, xp, kernels, sums, shift_ops, perm)


def parent_order(parent_bits):
    count = 2**parent_bits
    held = np.arange(count).reshape(-1, 8)[grid_permutation(parent_bits - 3)].T.reshape(-1)
    place = np.zeros(count, np.int64)
    place[held] = np.arange(count)
    perm = np.zeros((count, count), np.float32)
    perm[np.arange(count), place[grid_permutation(parent_bits)]] = 1
    return perm


def on_device(fine_mult, parent_mult, fine_mask, parent_mask, kernels, shift_ops):
    device_bits = lax.axis_size("box").bit_length() - 1
    device_index = lax.axis_index("box")
    fine_bits = fine_mult.shape[0].bit_length() - 1
    parent_bits = parent_mult.shape[0].bit_length() - 1
    width = fine_mult.shape[1]
    words = fine_mask.shape[0]
    fine = octant_grids(fine_mult, fine_bits)
    parent = octant_grids(parent_mult, parent_bits)
    F = fine_mult.shape[0] // 8
    G = parent_mult.shape[0] // 8
    n1, n2, n3 = fine.shape[1:4]
    m1, m2, m3 = parent.shape[1:4]
    masks = jnp.concatenate(
        [
            octant_grids(fine_mask.T, fine_bits).reshape(8, F, words),
            octant_grids(parent_mask.T, parent_bits).reshape(8, G, words),
        ],
        axis=1,
    )
    held = spread_masks(masks)
    for dim in (1, 2):
        fine, parent = exchange(fine, parent, dim, fine_bits, device_index, device_bits)
    is_odd = parity(0, fine_bits, device_index, device_bits)
    top = packed_face(fine, parent, 1, True)
    bottom = packed_face(fine, parent, 1, False)
    both = lax.all_gather(
        jnp.where(is_odd, top, bottom), "box", axis_index_groups=odd_groups(0, fine_bits, device_bits)
    )
    odd_got = jnp.where(is_odd, both[1], both[0])
    even_got = lax.ppermute(
        jnp.where(is_odd, bottom, top), "box", pair_route(0, 0, fine_bits, device_bits)
    )
    split = (n2 + 2) * (n3 + 2)

    def slab(got):
        return got[:, :split].reshape(8, 1, n2 + 2, n3 + 2, width)

    def parent_slab(got):
        return got[:, split:].reshape(8, 1, m2 + 2, m3 + 2, width)

    def across(block, w2, w3):
        return jnp.stack(
            [
                block[:, :, b : b + w2, c : c + w3].reshape(8, -1, width)
                for b in range(3)
                for c in range(3)
            ]
        )

    def moved_parents(got, goes_up):
        slab_got = parent_slab(got)
        up = jnp.concatenate([parent[:, 1:], slab_got], axis=1)
        down = jnp.concatenate([slab_got, parent[:, : m1 - 1]], axis=1)
        return across(jnp.where(goes_up, up, down), m2, m3)

    even = slab(even_got)
    x_even = across(jnp.concatenate([even, fine, even], axis=1), n2, n3)
    xp_even = jnp.concatenate(
        [across(parent, m2, m3), moved_parents(even_got, jnp.logical_not(is_odd))]
    ).reshape(-1, G, width)
    lists = shift_lists()
    slots = [126, 72]
    tables = []
    for odd in (False, True):
        near_side, far_side = (0, 2) if odd else (2, 0)
        tables.append(
            (
                work_table([lists[1], lists[near_side]], slots[0], n1 + 2, n2 * n3),
                work_table([lists[far_side]], slots[1], n1 + 2, n2 * n3),
            )
        )
    first_table = jnp.where(is_odd, tables[1][0], tables[0][0])
    last_table = jnp.where(is_odd, tables[1][1], tables[0][1])
    sums = first_terms(first_table, slots[0], held, x_even.reshape(-1, width), xp_even, kernels)
    odd_across = across(slab(odd_got), n2, n3)
    slab_rows = n2 * n3
    x_odd = lax.dynamic_update_slice(x_even, odd_across, (0, 0, 0, 0))
    x_odd = lax.dynamic_update_slice(x_odd, odd_across, (0, 0, (n1 + 1) * slab_rows, 0))
    xp_odd = moved_parents(odd_got, is_odd).reshape(-1, G, width)
    fine_local, parent_local = last_terms(
        last_table,
        slots[1],
        held,
        x_odd.reshape(-1, width),
        xp_odd,
        kernels,
        sums,
        shift_ops,
        jnp.asarray(parent_order(parent_bits), jnp.bfloat16),
    )
    fine_local = from_octants(fine_local, fine_bits)
    parent_local = from_octants(parent_local.reshape(8, G, width), parent_bits)
    return fine_local, parent_local


def from_octants(blocks, total_bits):
    width = blocks.shape[-1]
    bits = total_bits - 3
    axes_order, _ = grid_order(bits)
    grid = blocks.reshape((8,) + (2,) * bits + (width,))
    inverse = [0] * bits
    for position, source in enumerate(axes_order):
        inverse[source] = position
    moved = jnp.transpose(grid, tuple(1 + v for v in inverse) + (0, bits + 1))
    return moved.reshape(2**total_bits, width)


def solution(mesh):
    return jax.shard_map(
        on_device,
        mesh=mesh,
        in_specs=(P("box", None), P("box", None), P(None, "box"), P(None, "box"), P(), P()),
        out_specs=(P("box", None), P("box", None)),
        check_vma=False,
    )
```

time: 93.2 us -> 81.8 us (0.88)
  the two profiles are of different devices: /device:TPU:169 before, /device:TPU:58 now
where the time goes in v1:
time: 81.8 us; the launch traced here: 81.5 us
  Pallas kernels  34.1 us (42%)
  blocking collectives  17.6 us (22%)
  waiting for transfers between devices  11.5 us (14%)
  local copies, waits for them, and re-layouts  8.44 us (10%)
  starting transfers between devices  7.98 us (10%)
  between operations  1.37 us (2%)
    pallas_call x1, Pallas kernels, first_terms(): pl.pallas_call(kernel, out_shape=jax.ShapeDtypeStruct((8, rows, width), j...  19 us
    all_gather x1, blocking collectives, on_device(): lax.all_gather(jnp.where(is_odd, top, bottom), 'box', axis_index_groups=o...  17.6 us
    pallas_call x1, Pallas kernels, last_terms(): pl.pallas_call(kernel, out_shape=(jax.ShapeDtypeStruct((8, F, width), jnp...  11.4 us
    ppermute x1, waiting for transfers between devices, on_device(): lax.ppermute(jnp.where(is_odd, bottom, top), 'box', pair_route(0, 0, fine...  5.77 us
    ppermute x2, starting transfers between devices, exchange(): lax.ppermute(odd_send, 'box', pair_route(dim, 1, low_bits, device_bits))  5.59 us
    ppermute x2, waiting for transfers between devices, exchange(): lax.ppermute(odd_send, 'box', pair_route(dim, 1, low_bits, device_bits))  4.91 us
    pallas_call x1, Pallas kernels, spread_masks(): pl.pallas_call(kernel, out_shape=jax.ShapeDtypeStruct((words, 8, rows, 12...  3.82 us
    unnamed x63, local copies, waits for them, and re-layouts  3.69 us
  transfers between devices with their start and end apart: 5, of which 3 were waited for; matrix products, arithmetic and copies ran while one was open for 2% of the time, Pallas kernels for 5%

profile of v1, /device:TPU:58, one launch (start us, length us, event | category | flops | bytes accessed | tf_op | source)
XLA Modules:
  0.0 81.5 jit_solution(11461445854561118422)
XLA Ops:
  0.7 0.8 copy.202
  1.5 1.0 %copy.201 = bf16[2,2,2,2,2,2,2,8,128]{8,7,6,5,4,3,2,1,0:T(8,128)(2,1)S(1)} copy(bf16[2,2,2,2,2,2,2,8,128]{8,7,6,3,1,5,2,0,4:T(8,128)(2,1)} %bitcast.194) | data formatting | bytes 524288 | tf_op jit(solution)/shard_map/transpose | solution.py:41
  2.5 0.1 collective-permute-start
  2.6 2.7 %collective-permute-start.1 = (bf16[8,40,128]{2,0,1:T(8,128)(2,1)S(1)}, bf16[8,40,128]{2,0,1:T(8,128)(2,1)S(1)}, u32[]{:S(2)}, u32[]{:S(2)}) collective-permute-start(bf16[8,40,128]{2,0,1:T(8,128)(2,1)S(1)} %get-tuple-element.24), channel_id=1, source_target_pairs={{1,8},{3,10},{5,12},{7,14},{8,1},{9,64},{10,3},{11,66},{12,5},{13,... | collective-permute-start | bytes 245768 | tf_op jit(solution)/shard_map/ppermute | solution.py:96
  5.4 1.1 %copy.195 = s32[20,1024]{0,1:T(8,128)S(1)} copy(s32[20,1024]{1,0:T(8,128)} %param.13) | data formatting | bytes 163840 | tf_op args[2]
  6.5 0.1 copy.197
  6.7 0.1 copy.198
  6.9 3.8 %spread.1.words = s16[20,8,144,128]{3,2,1,0:T(8,128)(2,1)S(1)} custom-call(s32[8,144,20]{2,1,0:T(8,128)S(1)} %pad_add_fusion.packed), custom_call_target="tpu_custom_call" | custom-call | tf_op jit(solution)/shard_map/spread/pallas_call | solution.py:165
  10.9 2.2 %collective-permute-start.2 = (bf16[8,32,128]{2,0,1:T(8,128)(2,1)S(1)}, bf16[8,32,128]{2,0,1:T(8,128)(2,1)S(1)}, u32[]{:S(2)}, u32[]{:S(2)}) collective-permute-start(bf16[8,32,128]{2,0,1:T(8,128)(2,1)S(1)} %get-tuple-element.27), channel_id=1, source_target_pairs={{0,4},{1,5},{2,6},{3,7},{4,0},{5,1},{6,2},{7,3},{8,12},{9,13},{10,... | collective-permute-start | bytes 196616 | tf_op jit(solution)/shard_map/ppermute | solution.py:97
  13.1 2.8 %collective-permute-start.3 = (bf16[8,32,128]{2,0,1:T(8,128)(2,1)S(1)}, bf16[8,32,128]{2,0,1:T(8,128)(2,1)S(1)}, u32[]{:S(2)}, u32[]{:S(2)}) collective-permute-start(bf16[8,32,128]{2,0,1:T(8,128)(2,1)S(1)} %get-tuple-element.28), channel_id=1, source_target_pairs={{4,32},{5,33},{6,34},{7,35},{12,40},{13,41},{14,42},{15,43},{20,48... | collective-permute-start | bytes 196616 | tf_op jit(solution)/shard_map/ppermute | solution.py:96
  16.0 0.8 collective-permute-done.2
  16.8 4.9 %collective-permute-done.3 = bf16[8,32,128]{2,0,1:T(8,128)(2,1)S(1)} collective-permute-done((bf16[8,32,128]{2,0,1:T(8,128)(2,1)S(1)}, bf16[8,32,128]{2,0,1:T(8,128)(2,1)S(1)}, u32[]{:S(2)}, u32[]{:S(2)}) %collective-permute-start.3) | collective-permute-done | bytes 65568 | tf_op jit(solution)/shard_map/ppermute | solution.py:96
  21.9 17.6 %all_gather.4 = bf16[2,8,84,128]{3,1,2,0:T(8,128)(2,1)S(1)} all-gather(bf16[1,8,84,128]{3,1,2,0:T(8,128)(2,1)S(1)} %maximum_select_fusion.1), channel_id=1, replica_groups={{2,16},{3,17},{6,20},{7,21},{10,24},{11,25},{14,28},{15,29},{18,128},{1..., dimensions={0}, use_global_device_ids=true | all-gather | bytes 516096 | tf_op jit(solution)/shard_map/all_gather | solution.py:285
  39.6 0.1 collective-permute-start.4
  40.3 5.8 %collective-permute-done.4 = bf16[8,84,128]{2,0,1:T(8,128)(2,1)S(1)} collective-permute-done((bf16[8,84,128]{2,0,1:T(8,128)(2,1)S(1)}, bf16[8,84,128]{2,0,1:T(8,128)(2,1)S(1)}, u32[]{:S(2)}, u32[]{:S(2)}) %collective-permute-start.4) | collective-permute-done | bytes 172064 | tf_op jit(solution)/shard_map/ppermute | solution.py:289
  46.1 0.1 fusion.6
  46.2 0.2 pad_maximum_fusion
  46.4 0.6 fusion.3
  47.2 0.1 copy_dynamic-update-slice_fusion.7
  47.3 0.1 copy_dynamic-update-slice_fusion.6
  47.4 0.1 copy_dynamic-update-slice_fusion.5
  47.5 0.1 copy_dynamic-update-slice_fusion.4
  47.6 0.1 copy_dynamic-update-slice_fusion.3
  47.7 0.1 copy_dynamic-update-slice_fusion.2
  47.8 0.1 copy_dynamic-update-slice_fusion.1
  47.9 0.1 copy_dynamic-update-slice_fusion
  48.0 0.4 slice-done.1
  48.4 0.8 %slice-done.2 = s8[1966080]{0:T(1024)(128)(4,1)S(1)} async-done(((s8[10354688]{0:T(1024)(128)(4,1)}), s8[1966080]{0:T(1024)(128)(4,1)S(1)}, s32[]{:S(2)}) %slice-start.2) | async-done | bytes 1966104
  49.2 19.0 %first_terms.1.sums = f32[8,144,128]{2,1,0:T(8,128)S(1)} custom-call(s32[5,1008]{1,0:T(8,128)S(1)} %broadcast_select_fusion.8.table, s16[20,8,144,128]{3,2,1,0:T(8,128)(2,1)S(1)} %spread.1.words, bf16[13824,128]{1,0:T(8,128)(2,1)S(1)} %bitcast.128, bf16[144,16,128]{2,1,0:T(8,128)(2,1)S(1)} %bitcast.130, bf16[316,128,128]{2,1,0:T(8,128)(2,1)S(1)} %bitcast.127), custom_call_target="tpu_custom_call" | custom-call | tf_op jit(solution)/shard_map/first_terms/pallas_call | solution.py:208
  68.5 11.4 %last_terms.1 = (bf16[8,128,128]{2,1,0:T(8,128)(2,1)S(1)}, bf16[128,128]{1,0:T(8,128)(2,1)S(1)}) custom-call(s32[5,576]{1,0:T(8,128)S(1)} %broadcast_select_fusion.9.table, s16[20,8,144,128]{3,2,1,0:T(8,128)(2,1)S(1)} %spread.1.words, bf16[13824,128]{1,0:T(8,128)(2,1)S(1)} %bitcast.129, bf16[72,16,128]{2,1,0:T(8,128)(2,1)S(1)} %bitcast.131, ...), custom_call_target="tpu_custom_call" | custom-call | tf_op jit(solution)/shard_map/last_terms/pallas_call | solution.py:235
  79.9 1.0 %copy.254 = bf16[2,2,2,2,2,2,2,8,128]{8,7,6,5,4,3,2,1,0:T(8,128)(2,1)} copy(bf16[2,2,2,2,2,2,2,8,128]{8,6,3,0,5,2,4,1,7:T(2,128)(2,1)S(1)} %bitcast.132) | data formatting | bytes 524288 | tf_op jit(solution)/shard_map/transpose | solution.py:363
  80.9 0.6 copy.255
  (97 shorter events, 1.5 us)
Async XLA Ops:
  0.6 6.2 %copy-start.2 = (s32[5,1008]{1,0:T(8,128)S(1)}, s32[5,1008]{1,0:T(8,128)}, u32[]{:S(2)}) copy-start(s32[5,1008]{1,0:T(8,128)} %constant.22.clone) | copy-start | bytes 60484
  0.6 6.2 %copy-start.3 = (s32[5,1008]{1,0:T(8,128)S(1)}, s32[5,1008]{1,0:T(8,128)}, u32[]{:S(2)}) copy-start(s32[5,1008]{1,0:T(8,128)} %constant.23.clone) | copy-start | bytes 60484
  0.7 6.2 %copy-start.4 = (s32[5,576]{1,0:T(8,128)S(1)}, s32[5,576]{1,0:T(8,128)}, u32[]{:S(2)}) copy-start(s32[5,576]{1,0:T(8,128)} %constant.24.clone) | copy-start | bytes 34564
  0.7 6.2 %copy-start.5 = (s32[5,576]{1,0:T(8,128)S(1)}, s32[5,576]{1,0:T(8,128)}, u32[]{:S(2)}) copy-start(s32[5,576]{1,0:T(8,128)} %constant.25.clone) | copy-start | bytes 34564
  0.7 6.0 %copy-start.6 = (s32[20,128]{1,0:T(8,128)S(1)}, s32[20,128]{1,0:T(8,128)}, u32[]{:S(2)}) copy-start(s32[20,128]{1,0:T(8,128)} %param.14) | copy-start | bytes 30724
  2.5 8.2 %collective-permute-start = (bf16[8,40,128]{2,0,1:T(8,128)(2,1)S(1)}, bf16[8,40,128]{2,0,1:T(8,128)(2,1)S(1)}, u32[]{:S(2)}, u32[]{:S(2)}) collective-permute-start(bf16[8,40,128]{2,0,1:T(8,128)(2,1)S(1)} %get-tuple-element.23), channel_id=1, source_target_pairs={{0,1},{1,0},{2,3},{3,2},{4,5},{5,4},{6,7},{7,6},{8,9},{9,8},{10,11... | collective-permute-start | bytes 245768 | tf_op jit(solution)/shard_map/ppermute | solution.py:97
  2.6 8.2 %collective-permute-start.1 = (bf16[8,40,128]{2,0,1:T(8,128)(2,1)S(1)}, bf16[8,40,128]{2,0,1:T(8,128)(2,1)S(1)}, u32[]{:S(2)}, u32[]{:S(2)}) collective-permute-start(bf16[8,40,128]{2,0,1:T(8,128)(2,1)S(1)} %get-tuple-element.24), channel_id=1, source_target_pairs={{1,8},{3,10},{5,12},{7,14},{8,1},{9,64},{10,3},{11,66},{12,5},{13,... | collective-permute-start | bytes 245768 | tf_op jit(solution)/shard_map/ppermute | solution.py:96
  10.9 5.9 %collective-permute-start.2 = (bf16[8,32,128]{2,0,1:T(8,128)(2,1)S(1)}, bf16[8,32,128]{2,0,1:T(8,128)(2,1)S(1)}, u32[]{:S(2)}, u32[]{:S(2)}) collective-permute-start(bf16[8,32,128]{2,0,1:T(8,128)(2,1)S(1)} %get-tuple-element.27), channel_id=1, source_target_pairs={{0,4},{1,5},{2,6},{3,7},{4,0},{5,1},{6,2},{7,3},{8,12},{9,13},{10,... | collective-permute-start | bytes 196616 | tf_op jit(solution)/shard_map/ppermute | solution.py:97
  13.1 8.6 %collective-permute-start.3 = (bf16[8,32,128]{2,0,1:T(8,128)(2,1)S(1)}, bf16[8,32,128]{2,0,1:T(8,128)(2,1)S(1)}, u32[]{:S(2)}, u32[]{:S(2)}) collective-permute-start(bf16[8,32,128]{2,0,1:T(8,128)(2,1)S(1)} %get-tuple-element.28), channel_id=1, source_target_pairs={{4,32},{5,33},{6,34},{7,35},{12,40},{13,41},{14,42},{15,43},{20,48... | collective-permute-start | bytes 196616 | tf_op jit(solution)/shard_map/ppermute | solution.py:96
  39.5 8.4 %slice-start = ((s8[10354688]{0:T(1024)(128)(4,1)}), s8[4194304]{0:T(1024)(128)(4,1)S(1)}, s32[]{:S(2)}) async-start(s8[10354688]{0:T(1024)(128)(4,1)} %bitcast.126), calls=%async_computation | async-start | bytes 8388608
  39.6 6.4 %collective-permute-start.4 = (bf16[8,84,128]{2,0,1:T(8,128)(2,1)S(1)}, bf16[8,84,128]{2,0,1:T(8,128)(2,1)S(1)}, u32[]{:S(2)}, u32[]{:S(2)}) collective-permute-start(bf16[8,84,128]{2,0,1:T(8,128)(2,1)S(1)} %maximum_select_fusion), channel_id=1, source_target_pairs={{0,2},{1,3},{2,0},{3,1},{4,6},{5,7},{6,4},{7,5},{8,10},{9,11},{10,... | collective-permute-start | bytes 516104 | tf_op jit(solution)/shard_map/ppermute | solution.py:289
  46.2 2.2 %slice-start.1 = ((s8[10354688]{0:T(1024)(128)(4,1)}), s8[4194304]{0:T(1024)(128)(4,1)S(1)}, s32[]{:S(2)}) async-start(s8[10354688]{0:T(1024)(128)(4,1)} %bitcast.126), calls=%async_computation.1 | async-start | bytes 8388608
  47.0 2.2 %slice-start.2 = ((s8[10354688]{0:T(1024)(128)(4,1)}), s8[1966080]{0:T(1024)(128)(4,1)S(1)}, s32[]{:S(2)}) async-start(s8[10354688]{0:T(1024)(128)(4,1)} %bitcast.126), calls=%async_computation.2 | async-start | bytes 3932160
  49.2 19.3 %copy-start = (bf16[8,128,128]{2,1,0:T(8,128)(2,1)S(1)}, bf16[8,128,128]{2,1,0:T(8,128)(2,1)}, u32[]{:S(2)}) copy-start(bf16[8,128,128]{2,1,0:T(8,128)(2,1)} %shift.1) | copy-start | bytes 786436
  49.2 19.3 %copy-start.1 = (bf16[128,128]{1,0:T(8,128)(2,1)S(1)}, bf16[128,128]{1,0:T(8,128)(2,1)}, u32[]{:S(2)}) copy-start(bf16[128,128]{1,0:T(8,128)(2,1)} %constant.26.clone.perm) | copy-start | bytes 98308

commit v2 on v1

--- a/solution.py
+++ b/solution.py
@@ -107,14 +107,6 @@
     return out
 
 
-def odd_groups(dim, low_bits, device_bits):
-    paired = pair_route(dim, 1, low_bits, device_bits)
-    groups = [[a, b] for a, b in paired if a < b]
-    seen = {a for a, _ in paired}
-    rest = [number for number in range(2**device_bits) if number not in seen]
-    return groups + [[rest[k], rest[k + 1]] for k in range(0, len(rest), 2)]
-
-
 def shift_lists():
     offsets = direction_table()
     lists = [[[] for _ in range(8)] for _ in range(3)]
@@ -135,6 +127,7 @@
 
 def work_table(groups, slots, slab_count, slab_rows):
     table = np.zeros((5, 8, slots), np.int32)
+    table[3] = -1
     for octant in range(8):
         at = 0
         for place, per_octant in enumerate(groups):
@@ -143,66 +136,68 @@
                 table[0, octant, at] = number
                 table[1, octant, at] = (across * 8 + source) * slab_count * slab_rows + shift[0] * slab_rows
                 table[2, octant, at] = (place * 9 + across) * 8 + source
-                table[3, octant, at] = number // 16
-                table[4, octant, at] = 1 << (number % 16)
+                table[3, octant, at] = number // 8
+                table[4, octant, at] = number % 8
                 at += 1
-    return table.reshape(5, 8 * slots)
-
-
-def spread_masks(masks):
-    rows, words = masks.shape[1:]
-
-    def kernel(packed, out):
+    return table
+
+
+def unpack_masks(packed, byte_of, shift_of):
+    octants, rows, count = packed.shape
+    chunks = byte_of.shape[0]
+
+    def kernel(packed, byte_of, shift_of, out):
         def one(octant, carry):
-            for w in range(words):
-                column = packed[octant, :, w : w + 1]
-                out[w, octant] = jnp.broadcast_to(column, (rows, 128)).astype(jnp.int16)
+            lines = lax.broadcasted_iota(jnp.int32, (count, 128), 0)
+            for c in range(chunks):
+                pick = (lines == byte_of[c, pl.ds(octant, 1), :]).astype(jnp.float32).astype(jnp.bfloat16)
+                value = jnp.dot(packed[octant], pick, preferred_element_type=jnp.float32).astype(jnp.int32)
+                bit = jnp.right_shift(value, jnp.broadcast_to(shift_of[c, pl.ds(octant, 1), :], value.shape)) & 1
+                out[c, octant] = bit.astype(jnp.float32)
             return carry
 
-        lax.fori_loop(0, 8, one, 0)
+        lax.fori_loop(0, octants, one, 0)
 
     vmem = pl.BlockSpec(memory_space=pltpu.VMEM)
     return pl.pallas_call(
         kernel,
-        out_shape=jax.ShapeDtypeStruct((words, 8, rows, 128), jnp.int16),
-        in_specs=[vmem],
+        out_shape=jax.ShapeDtypeStruct((chunks, octants, rows, 128), jnp.float32),
+        in_specs=[vmem] * 3,
         out_specs=vmem,
         compiler_params=pltpu.CompilerParams(vmem_limit_bytes=16 << 20),
-        name="spread",
-    )(masks)
-
-
-def add_terms(table, slots, words, x, xp, kernels, acc):
+        name="unpack",
+    )(packed, byte_of, shift_of)
+
+
+def add_terms(table, slots, first, masks, x, xp, kernels, acc):
     F = acc.shape[1] - xp.shape[1]
     rows = acc.shape[1]
 
-    def masked(octant, at):
-        place = octant * slots + at
-        wanted = jnp.broadcast_to(table[4, place], (16, 128)).astype(jnp.int16)
-        wanted = jnp.broadcast_to(wanted[:1], (rows, 128))
+    def masked(place, column):
         row = pl.multiple_of(table[1, place], 16)
         value = jnp.concatenate([x[pl.ds(row, F), :], xp[table[2, place]]], axis=0)
-        held = words[table[3, place], octant]
-        return jnp.where((held & wanted) != 0, value, jnp.zeros_like(value))
+        return value * jnp.broadcast_to(column, (rows, 128)).astype(jnp.bfloat16)
 
     def step(number, carry):
         at = number * CHUNK
         for octant in range(8):
-            left = jnp.concatenate([masked(octant, at + j) for j in range(CHUNK)], axis=1)
-            right = jnp.concatenate([kernels[table[0, octant * slots + at + j]] for j in range(CHUNK)], axis=0)
+            place = octant * slots + at
+            columns = masks[first + number, octant]
+            left = jnp.concatenate([masked(place + j, columns[:, j : j + 1]) for j in range(CHUNK)], axis=1)
+            right = jnp.concatenate([kernels[table[0, place + j]] for j in range(CHUNK)], axis=0)
             acc[octant] += jnp.dot(left, right, preferred_element_type=jnp.float32)
         return carry
 
     lax.fori_loop(0, slots // CHUNK, step, 0)
 
 
-def first_terms(table, slots, words, x, xp, kernels):
-    rows = words.shape[2]
+def first_terms(table, slots, masks, x, xp, kernels):
+    rows = masks.shape[2]
     width = kernels.shape[1]
 
-    def kernel(table, words, x, xp, kernels, acc):
+    def kernel(table, masks, x, xp, kernels, acc):
         acc[...] = jnp.zeros_like(acc)
-        add_terms(table, slots, words, x, xp, kernels, acc)
+        add_terms(table, slots, 0, masks, x, xp, kernels, acc)
 
     vmem = pl.BlockSpec(memory_space=pltpu.VMEM)
     return pl.pallas_call(
@@ -211,18 +206,21 @@
         in_specs=[pl.BlockSpec(memory_space=pltpu.SMEM)] + [vmem] * 4,
         out_specs=vmem,
         compiler_params=pltpu.CompilerParams(vmem_limit_bytes=16 << 20),
+        cost_estimate=pl.CostEstimate(
+            flops=2 * 8 * rows * slots * width * width, transcendentals=0, bytes_accessed=x.size * 2
+        ),
         name="first_terms",
-    )(table, words, x, xp, kernels)
-
-
-def last_terms(table, slots, words, x, xp, kernels, sums, shift_ops, perm):
-    rows = words.shape[2]
+    )(table, masks, x, xp, kernels)
+
+
+def last_terms(table, slots, first, masks, x, xp, kernels, sums, shift_ops, perm):
+    rows = masks.shape[2]
     width = kernels.shape[1]
     F = perm.shape[0]
 
-    def kernel(table, words, x, xp, kernels, sums, shift, perm, fine_out, parent_out, acc):
+    def kernel(table, masks, x, xp, kernels, sums, shift, perm, fine_out, parent_out, acc):
         acc[...] = sums[...]
-        add_terms(table, slots, words, x, xp, kernels, acc)
+        add_terms(table, slots, first, masks, x, xp, kernels, acc)
         far = [(acc[p, F:, :] * 0.5).astype(jnp.bfloat16) for p in range(8)]
         local = jnp.concatenate(far, axis=0)
         parent_out[...] = local
@@ -243,7 +241,7 @@
         scratch_shapes=[pltpu.VMEM((8, rows, width), jnp.float32)],
         compiler_params=pltpu.CompilerParams(vmem_limit_bytes=16 << 20),
         name="last_terms",
-    )(table, words, x, xp, kernels, sums, shift_ops, perm)
+    )(table, masks, x, xp, kernels, sums, shift_ops, perm)
 
 
 def parent_order(parent_bits):
@@ -276,47 +274,7 @@
         ],
         axis=1,
     )
-    held = spread_masks(masks)
-    for dim in (1, 2):
-        fine, parent = exchange(fine, parent, dim, fine_bits, device_index, device_bits)
     is_odd = parity(0, fine_bits, device_index, device_bits)
-    top = packed_face(fine, parent, 1, True)
-    bottom = packed_face(fine, parent, 1, False)
-    both = lax.all_gather(
-        jnp.where(is_odd, top, bottom), "box", axis_index_groups=odd_groups(0, fine_bits, device_bits)
-    )
-    odd_got = jnp.where(is_odd, both[1], both[0])
-    even_got = lax.ppermute(
-        jnp.where(is_odd, bottom, top), "box", pair_route(0, 0, fine_bits, device_bits)
-    )
-    split = (n2 + 2) * (n3 + 2)
-
-    def slab(got):
-        return got[:, :split].reshape(8, 1, n2 + 2, n3 + 2, width)
-
-    def parent_slab(got):
-        return got[:, split:].reshape(8, 1, m2 + 2, m3 + 2, width)
-
-    def across(block, w2, w3):
-        return jnp.stack(
-            [
-                block[:, :, b : b + w2, c : c + w3].reshape(8, -1, width)
-                for b in range(3)
-                for c in range(3)
-            ]
-        )
-
-    def moved_parents(got, goes_up):
-        slab_got = parent_slab(got)
-        up = jnp.concatenate([parent[:, 1:], slab_got], axis=1)
-        down = jnp.concatenate([slab_got, parent[:, : m1 - 1]], axis=1)
-        return across(jnp.where(goes_up, up, down), m2, m3)
-
-    even = slab(even_got)
-    x_even = across(jnp.concatenate([even, fine, even], axis=1), n2, n3)
-    xp_even = jnp.concatenate(
-        [across(parent, m2, m3), moved_parents(even_got, jnp.logical_not(is_odd))]
-    ).reshape(-1, G, width)
     lists = shift_lists()
     slots = [126, 72]
     tables = []
@@ -328,9 +286,62 @@
                 work_table([lists[far_side]], slots[1], n1 + 2, n2 * n3),
             )
         )
-    first_table = jnp.where(is_odd, tables[1][0], tables[0][0])
-    last_table = jnp.where(is_odd, tables[1][1], tables[0][1])
+
+    def by_parity(make):
+        return jnp.where(is_odd, make(tables[1]), make(tables[0]))
+
+    def columns(line):
+        def make(pair):
+            joined = np.concatenate([pair[0][line], pair[1][line]], axis=1)
+            chunked = joined.reshape(8, -1, CHUNK).transpose(1, 0, 2)
+            return np.pad(chunked, ((0, 0), (0, 0), (0, 128 - CHUNK)))
+
+        return by_parity(make)
+
+    first_table = by_parity(lambda pair: pair[0][:3].reshape(3, -1))
+    last_table = by_parity(lambda pair: pair[1][:3].reshape(3, -1))
+    packed = jnp.stack([masks & 255, jnp.right_shift(masks, 8)], axis=3).astype(jnp.bfloat16)
+    held = unpack_masks(packed.reshape(8, F + G, 2 * words), columns(3), columns(4))
+    for dim in (1, 2):
+        fine, parent = exchange(fine, parent, dim, fine_bits, device_index, device_bits)
+    top = packed_face(fine, parent, 1, True)
+    bottom = packed_face(fine, parent, 1, False)
+    even_got = lax.ppermute(
+        jnp.where(is_odd, bottom, top), "box", pair_route(0, 0, fine_bits, device_bits)
+    )
+    odd_got = lax.ppermute(
+        jnp.where(is_odd, top, bottom), "box", pair_route(0, 1, fine_bits, device_bits)
+    )
+    split = (n2 + 2) * (n3 + 2)
+
+    def slab(got):
+        return got[:, :split].reshape(8, 1, n2 + 2, n3 + 2, width)
+
+    def parent_slab(got):
+        return got[:, split:].reshape(8, 1, m2 + 2, m3 + 2, width)
+
+    def across(block, w2, w3):
+        return jnp.stack(
+            [
+                block[:, :, b : b + w2, c : c + w3].reshape(8, -1, width)
+                for b in range(3)
+                for c in range(3)
+            ]
+        )
+
+    def moved_parents(got, goes_up):
+        slab_got = parent_slab(got)
+        up = jnp.concatenate([parent[:, 1:], slab_got], axis=1)
+        down = jnp.concatenate([slab_got, parent[:, : m1 - 1]], axis=1)
+        return across(jnp.where(goes_up, up, down), m2, m3)
+
+    even = slab(even_got)
+    x_even = across(jnp.concatenate([even, fine, even], axis=1), n2, n3)
+    xp_even = jnp.concatenate(
+        [across(parent, m2, m3), moved_parents(even_got, jnp.logical_not(is_odd))]
+    ).reshape(-1, G, width)
     sums = first_terms(first_table, slots[0], held, x_even.reshape(-1, width), xp_even, kernels)
+    sums, odd_got = lax.optimization_barrier((sums, odd_got))
     odd_across = across(slab(odd_got), n2, n3)
     slab_rows = n2 * n3
     x_odd = lax.dynamic_update_slice(x_even, odd_across, (0, 0, 0, 0))
@@ -339,6 +350,7 @@
     fine_local, parent_local = last_terms(
         last_table,
         slots[1],
+        slots[0] // CHUNK,
         held,
         x_odd.reshape(-1, width),
         xp_odd,

time: 81.8 us -> 62.9 us (0.77)
  the two profiles are of different devices: /device:TPU:58 before, /device:TPU:31 now
where the time goes in v2:
time: 62.9 us; the launch traced here: 62.3 us
  Pallas kernels  27 us (43%)
  starting transfers between devices  21.7 us (34%)
  local copies, waits for them, and re-layouts  9.15 us (15%)
  waiting for transfers between devices  2.39 us (4%)
  between operations  1.48 us (2%)
    pallas_call x1, Pallas kernels, first_terms(): pl.pallas_call(kernel, out_shape=jax.ShapeDtypeStruct((8, rows, width), j...  15 us
    ppermute x2, starting transfers between devices, exchange(): lax.ppermute(odd_send, 'box', pair_route(dim, 1, low_bits, device_bits))  10.1 us
    ppermute x1, starting transfers between devices, on_device(): lax.ppermute(jnp.where(is_odd, top, bottom), 'box', pair_route(0, 1, fine...  9.62 us
    pallas_call x1, Pallas kernels, last_terms(): pl.pallas_call(kernel, out_shape=(jax.ShapeDtypeStruct((8, F, width), jnp...  9.11 us
    unnamed x71, local copies, waits for them, and re-layouts  3.82 us
    pallas_call x1, Pallas kernels, unpack_masks(): pl.pallas_call(kernel, out_shape=jax.ShapeDtypeStruct((chunks, octants, r...  2.85 us
    ppermute x2, waiting for transfers between devices, exchange(): lax.ppermute(odd_send, 'box', pair_route(dim, 1, low_bits, device_bits))  2.38 us
    ppermute x2, starting transfers between devices, exchange(): lax.ppermute(even_send, 'box', pair_route(dim, 0, low_bits, device_bits))  1.96 us
  transfers between devices with their start and end apart: 6, of which 1 were waited for; matrix products, arithmetic and copies ran while one was open for 6% of the time, Pallas kernels for 29%

profile of v2, /device:TPU:31, one launch (start us, length us, event | category | flops | bytes accessed | tf_op | source)
XLA Modules:
  0.0 62.3 jit_solution(5583133337867559446)
XLA Ops:
  0.7 0.8 %copy.152 = bf16[2,2,2,2,8,128]{5,4,3,2,1,0:T(8,128)(2,1)S(1)} copy(bf16[2,2,2,2,8,128]{5,4,3,1,0,2:T(8,128)(2,1)} %bitcast.230) | data formatting | bytes 65536 | tf_op jit(solution)/shard_map/transpose | solution.py:41
  1.6 1.0 %copy.151 = bf16[2,2,2,2,2,2,2,8,128]{8,7,6,5,4,3,2,1,0:T(8,128)(2,1)S(1)} copy(bf16[2,2,2,2,2,2,2,8,128]{8,7,6,3,1,5,2,0,4:T(8,128)(2,1)} %bitcast.186) | data formatting | bytes 524288 | tf_op jit(solution)/shard_map/transpose | solution.py:41
  2.6 0.8 %collective-permute-start = (bf16[8,40,128]{2,0,1:T(8,128)(2,1)S(1)}, bf16[8,40,128]{2,0,1:T(8,128)(2,1)S(1)}, u32[]{:S(2)}, u32[]{:S(2)}) collective-permute-start(bf16[8,40,128]{2,0,1:T(8,128)(2,1)S(1)} %get-tuple-element.29), channel_id=1, source_target_pairs={{0,1},{1,0},{2,3},{3,2},{4,5},{5,4},{6,7},{7,6},{8,9},{9,8},{10,11... | collective-permute-start | bytes 245768 | tf_op jit(solution)/shard_map/ppermute | solution.py:97
  3.3 5.0 %collective-permute-start.1 = (bf16[8,40,128]{2,0,1:T(8,128)(2,1)S(1)}, bf16[8,40,128]{2,0,1:T(8,128)(2,1)S(1)}, u32[]{:S(2)}, u32[]{:S(2)}) collective-permute-start(bf16[8,40,128]{2,0,1:T(8,128)(2,1)S(1)} %get-tuple-element.30), channel_id=1, source_target_pairs={{1,8},{3,10},{5,12},{7,14},{8,1},{9,64},{10,3},{11,66},{12,5},{13,... | collective-permute-start | bytes 245768 | tf_op jit(solution)/shard_map/ppermute | solution.py:96
  8.3 1.1 %copy.143 = s32[20,1024]{0,1:T(8,128)S(1)} copy(s32[20,1024]{1,0:T(8,128)} %param.17) | data formatting | bytes 163840 | tf_op args[2]
  9.5 0.2 copy.148
  9.8 0.1 copy.146
  9.9 0.1 copy.149
  10.2 0.2 copy.150.packed
  10.5 2.8 %unpack.1.masks = f32[11,8,144,128]{3,2,1,0:T(8,128)S(1)} custom-call(bf16[8,144,40]{2,1,0:T(8,128)(2,1)S(1)} %copy.150.packed, s32[11,8,128]{2,1,0:T(8,128)S(1)} %get-tuple-element.81.byte_of, s32[11,8,128]{2,1,0:T(8,128)S(1)} %get-tuple-element.80.shift_of), custom_call_target="tpu_custom_call" | custom-call | tf_op jit(solution)/shard_map/unpack/pallas_call | solution.py:162
  13.5 1.2 %collective-permute-start.2 = (bf16[8,32,128]{2,0,1:T(8,128)(2,1)S(1)}, bf16[8,32,128]{2,0,1:T(8,128)(2,1)S(1)}, u32[]{:S(2)}, u32[]{:S(2)}) collective-permute-start(bf16[8,32,128]{2,0,1:T(8,128)(2,1)S(1)} %get-tuple-element.35), channel_id=1, source_target_pairs={{0,4},{1,5},{2,6},{3,7},{4,0},{5,1},{6,2},{7,3},{8,12},{9,13},{10,... | collective-permute-start | bytes 196616 | tf_op jit(solution)/shard_map/ppermute | solution.py:97
  14.7 5.1 %collective-permute-start.3 = (bf16[8,32,128]{2,0,1:T(8,128)(2,1)S(1)}, bf16[8,32,128]{2,0,1:T(8,128)(2,1)S(1)}, u32[]{:S(2)}, u32[]{:S(2)}) collective-permute-start(bf16[8,32,128]{2,0,1:T(8,128)(2,1)S(1)} %get-tuple-element.36), channel_id=1, source_target_pairs={{4,32},{5,33},{6,34},{7,35},{12,40},{13,41},{14,42},{15,43},{20,48... | collective-permute-start | bytes 196616 | tf_op jit(solution)/shard_map/ppermute | solution.py:96
  19.8 2.4 %collective-permute-done.3 = bf16[8,32,128]{2,0,1:T(8,128)(2,1)S(1)} collective-permute-done((bf16[8,32,128]{2,0,1:T(8,128)(2,1)S(1)}, bf16[8,32,128]{2,0,1:T(8,128)(2,1)S(1)}, u32[]{:S(2)}, u32[]{:S(2)}) %collective-permute-start.3) | collective-permute-done | bytes 65568 | tf_op jit(solution)/shard_map/ppermute | solution.py:96
  22.5 0.1 collective-permute-start.4
  22.6 9.6 %collective-permute-start.5 = (bf16[8,84,128]{2,0,1:T(8,128)(2,1)S(1)}, bf16[8,84,128]{2,0,1:T(8,128)(2,1)S(1)}, u32[]{:S(2)}, u32[]{:S(2)}) collective-permute-start(bf16[8,84,128]{2,0,1:T(8,128)(2,1)S(1)} %get-tuple-element.23), channel_id=1, source_target_pairs={{2,16},{3,17},{6,20},{7,21},{10,24},{11,25},{14,28},{15,29},{16,2}... | collective-permute-start | bytes 516104 | tf_op jit(solution)/shard_map/ppermute | solution.py:312
  32.5 0.2 pad_maximum_fusion
  32.7 0.7 %fusion.2 = (bf16[8,6,4,8,128]{4,0,3,2,1:T(8,128)(2,1)S(1)}, bf16[8,6,4,8,128]{4,0,3,2,1:T(8,128)(2,1)S(1)}, bf16[8,6,4,8,128]{4,0,3,2,1:T(8,128)(2,1)S(1)}, bf1...) fusion(bf16[8,6,6,10,128]{4,0,3,2,1:T(8,128)(2,1)S(1)} %pad_max, ...), kind=kLoop, calls=%fused_computation.94 | loop fusion | bytes 7077888 | tf_op jit(solution)/shard_map/slice | solution.py:326
  33.6 0.1 copy_dynamic-update-slice_fusion.7
  33.7 0.1 copy_dynamic-update-slice_fusion.6
  33.8 0.1 copy_dynamic-update-slice_fusion.5
  33.9 0.1 copy_dynamic-update-slice_fusion.4
  34.0 0.1 copy_dynamic-update-slice_fusion.3
  34.1 0.1 copy_dynamic-update-slice_fusion.2
  34.2 0.1 copy_dynamic-update-slice_fusion.1
  34.3 0.1 copy_dynamic-update-slice_fusion
  34.4 0.3 slice-done.1
  34.7 0.8 %slice-done.2 = s8[1966080]{0:T(1024)(128)(4,1)S(1)} async-done(((s8[10354688]{0:T(1024)(128)(4,1)}), s8[1966080]{0:T(1024)(128)(4,1)S(1)}, s32[]{:S(2)}) %slice-start.2) | async-done | bytes 1966104
  35.6 15.0 %first_terms.1.sums = f32[8,144,128]{2,1,0:T(8,128)S(1)} custom-call(s32[3,1008]{1,0:T(4,128)S(1)} %broadcast_select_fusion.12.table, f32[11,8,144,128]{3,2,1,0:T(8,128)S(1)} %unpack.1.masks, bf16[13824,128]{1,0:T(8,128)(2,1)S(1)} %bitcast.125, bf16[144,16,128]{2,1,0:T(8,128)(2,1)S(1)} %bitcast.127, bf16[316,128,128]{2,1,0:T(8,128)(2,1)S(1)} %bitcast.124), custom_call_target="tpu_custom_call" | custom-call | flops 4756340736 | bytes 3538944 | tf_op jit(solution)/shard_map/first_terms/pallas_call | solution.py:203
  51.4 0.1 copy-done
  51.5 9.1 %last_terms.1 = (bf16[8,128,128]{2,1,0:T(8,128)(2,1)S(1)}, bf16[128,128]{1,0:T(8,128)(2,1)S(1)}) custom-call(s32[3,576]{1,0:T(4,128)S(1)} %broadcast_select_fusion.13.table, f32[11,8,144,128]{3,2,1,0:T(8,128)S(1)} %unpack.1.masks, bf16[13824,128]{1,0:T(8,128)(2,1)S(1)} %bitcast.126, bf16[72,16,128]{2,1,0:T(8,128)(2,1)S(1)} %bitcast.128, ...), custom_call_target="tpu_custom_call" | custom-call | tf_op jit(solution)/shard_map/last_terms/pallas_call | solution.py:233
  60.6 1.0 %copy.204 = bf16[2,2,2,2,2,2,2,8,128]{8,7,6,5,4,3,2,1,0:T(8,128)(2,1)} copy(bf16[2,2,2,2,2,2,2,8,128]{8,6,3,0,5,2,4,1,7:T(2,128)(2,1)S(1)} %bitcast.129) | data formatting | bytes 524288 | tf_op jit(solution)/shard_map/transpose | solution.py:375
  61.7 0.6 %copy.205 = bf16[2,2,2,2,8,128]{5,4,3,2,1,0:T(8,128)(2,1)} copy(bf16[2,2,2,2,8,128]{5,3,0,2,1,4:T(2,128)(2,1)S(1)} %bitcast.130) | data formatting | bytes 65536 | tf_op jit(solution)/shard_map/transpose | solution.py:375
  (109 shorter events, 1.6 us)
Async XLA Ops:
  0.6 9.4 %copy-start.6 = (s32[3,1008]{1,0:T(4,128)S(1)}, s32[3,1008]{1,0:T(4,128)}, u32[]{:S(2)}) copy-start(s32[3,1008]{1,0:T(4,128)} %constant.34.clone) | copy-start | bytes 36292
  0.6 9.4 %copy-start.7 = (s32[3,1008]{1,0:T(4,128)S(1)}, s32[3,1008]{1,0:T(4,128)}, u32[]{:S(2)}) copy-start(s32[3,1008]{1,0:T(4,128)} %constant.35.clone) | copy-start | bytes 36292
  0.7 9.4 %copy-start.9 = (s32[3,576]{1,0:T(4,128)S(1)}, s32[3,576]{1,0:T(4,128)}, u32[]{:S(2)}) copy-start(s32[3,576]{1,0:T(4,128)} %constant.36.clone) | copy-start | bytes 20740
  0.7 9.4 %copy-start.10 = (s32[3,576]{1,0:T(4,128)S(1)}, s32[3,576]{1,0:T(4,128)}, u32[]{:S(2)}) copy-start(s32[3,576]{1,0:T(4,128)} %constant.37.clone) | copy-start | bytes 20740
  0.7 9.4 %copy-start.2 = (s32[11,8,128]{2,1,0:T(8,128)S(1)}, s32[11,8,128]{2,1,0:T(8,128)}, u32[]{:S(2)}) copy-start(s32[11,8,128]{2,1,0:T(8,128)} %constant.38.clone) | copy-start | bytes 135172
  0.7 9.4 %copy-start.3 = (s32[11,8,128]{2,1,0:T(8,128)S(1)}, s32[11,8,128]{2,1,0:T(8,128)}, u32[]{:S(2)}) copy-start(s32[11,8,128]{2,1,0:T(8,128)} %constant.39.clone) | copy-start | bytes 135172
  0.7 9.4 %copy-start.4 = (s32[11,8,128]{2,1,0:T(8,128)S(1)}, s32[11,8,128]{2,1,0:T(8,128)}, u32[]{:S(2)}) copy-start(s32[11,8,128]{2,1,0:T(8,128)} %constant.40.clone) | copy-start | bytes 135172
  0.7 9.4 %copy-start.5 = (s32[11,8,128]{2,1,0:T(8,128)S(1)}, s32[11,8,128]{2,1,0:T(8,128)}, u32[]{:S(2)}) copy-start(s32[11,8,128]{2,1,0:T(8,128)} %constant.41.clone) | copy-start | bytes 135172
  0.7 9.0 %copy-start.8 = (s32[20,128]{1,0:T(8,128)S(1)}, s32[20,128]{1,0:T(8,128)}, u32[]{:S(2)}) copy-start(s32[20,128]{1,0:T(8,128)} %param.18) | copy-start | bytes 30724
  2.6 10.7 %collective-permute-start = (bf16[8,40,128]{2,0,1:T(8,128)(2,1)S(1)}, bf16[8,40,128]{2,0,1:T(8,128)(2,1)S(1)}, u32[]{:S(2)}, u32[]{:S(2)}) collective-permute-start(bf16[8,40,128]{2,0,1:T(8,128)(2,1)S(1)} %get-tuple-element.29), channel_id=1, source_target_pairs={{0,1},{1,0},{2,3},{3,2},{4,5},{5,4},{6,7},{7,6},{8,9},{9,8},{10,11... | collective-permute-start | bytes 245768 | tf_op jit(solution)/shard_map/ppermute | solution.py:97
  3.3 10.0 %collective-permute-start.1 = (bf16[8,40,128]{2,0,1:T(8,128)(2,1)S(1)}, bf16[8,40,128]{2,0,1:T(8,128)(2,1)S(1)}, u32[]{:S(2)}, u32[]{:S(2)}) collective-permute-start(bf16[8,40,128]{2,0,1:T(8,128)(2,1)S(1)} %get-tuple-element.30), channel_id=1, source_target_pairs={{1,8},{3,10},{5,12},{7,14},{8,1},{9,64},{10,3},{11,66},{12,5},{13,... | collective-permute-start | bytes 245768 | tf_op jit(solution)/shard_map/ppermute | solution.py:96
  13.4 21.0 %slice-start = ((s8[10354688]{0:T(1024)(128)(4,1)}), s8[4194304]{0:T(1024)(128)(4,1)S(1)}, s32[]{:S(2)}) async-start(s8[10354688]{0:T(1024)(128)(4,1)} %bitcast.123), calls=%async_computation | async-start | bytes 8388608
  13.5 6.3 %collective-permute-start.2 = (bf16[8,32,128]{2,0,1:T(8,128)(2,1)S(1)}, bf16[8,32,128]{2,0,1:T(8,128)(2,1)S(1)}, u32[]{:S(2)}, u32[]{:S(2)}) collective-permute-start(bf16[8,32,128]{2,0,1:T(8,128)(2,1)S(1)} %get-tuple-element.35), channel_id=1, source_target_pairs={{0,4},{1,5},{2,6},{3,7},{4,0},{5,1},{6,2},{7,3},{8,12},{9,13},{10,... | collective-permute-start | bytes 196616 | tf_op jit(solution)/shard_map/ppermute | solution.py:97
  14.7 7.5 %collective-permute-start.3 = (bf16[8,32,128]{2,0,1:T(8,128)(2,1)S(1)}, bf16[8,32,128]{2,0,1:T(8,128)(2,1)S(1)}, u32[]{:S(2)}, u32[]{:S(2)}) collective-permute-start(bf16[8,32,128]{2,0,1:T(8,128)(2,1)S(1)} %get-tuple-element.36), channel_id=1, source_target_pairs={{4,32},{5,33},{6,34},{7,35},{12,40},{13,41},{14,42},{15,43},{20,48... | collective-permute-start | bytes 196616 | tf_op jit(solution)/shard_map/ppermute | solution.py:96
  22.5 9.9 %collective-permute-start.4 = (bf16[8,84,128]{2,0,1:T(8,128)(2,1)S(1)}, bf16[8,84,128]{2,0,1:T(8,128)(2,1)S(1)}, u32[]{:S(2)}, u32[]{:S(2)}) collective-permute-start(bf16[8,84,128]{2,0,1:T(8,128)(2,1)S(1)} %get-tuple-element.24), channel_id=1, source_target_pairs={{0,2},{1,3},{2,0},{3,1},{4,6},{5,7},{6,4},{7,5},{8,10},{9,11},{10,... | collective-permute-start | bytes 516104 | tf_op jit(solution)/shard_map/ppermute | solution.py:309
  22.6 28.0 %collective-permute-start.5 = (bf16[8,84,128]{2,0,1:T(8,128)(2,1)S(1)}, bf16[8,84,128]{2,0,1:T(8,128)(2,1)S(1)}, u32[]{:S(2)}, u32[]{:S(2)}) collective-permute-start(bf16[8,84,128]{2,0,1:T(8,128)(2,1)S(1)} %get-tuple-element.23), channel_id=1, source_target_pairs={{2,16},{3,17},{6,20},{7,21},{10,24},{11,25},{14,28},{15,29},{16,2}... | collective-permute-start | bytes 516104 | tf_op jit(solution)/shard_map/ppermute | solution.py:312
  32.5 2.2 %slice-start.1 = ((s8[10354688]{0:T(1024)(128)(4,1)}), s8[4194304]{0:T(1024)(128)(4,1)S(1)}, s32[]{:S(2)}) async-start(s8[10354688]{0:T(1024)(128)(4,1)} %bitcast.123), calls=%async_computation.1 | async-start | bytes 8388608
  33.4 2.2 %slice-start.2 = ((s8[10354688]{0:T(1024)(128)(4,1)}), s8[1966080]{0:T(1024)(128)(4,1)S(1)}, s32[]{:S(2)}) async-start(s8[10354688]{0:T(1024)(128)(4,1)} %bitcast.123), calls=%async_computation.2 | async-start | bytes 3932160
  50.6 1.0 %copy-start = (bf16[8,128,128]{2,1,0:T(8,128)(2,1)S(1)}, bf16[8,128,128]{2,1,0:T(8,128)(2,1)}, u32[]{:S(2)}) copy-start(bf16[8,128,128]{2,1,0:T(8,128)(2,1)} %shift.1) | copy-start | bytes 786436
  50.6 0.9 %copy-start.1 = (bf16[128,128]{1,0:T(8,128)(2,1)S(1)}, bf16[128,128]{1,0:T(8,128)(2,1)}, u32[]{:S(2)}) copy-start(bf16[128,128]{1,0:T(8,128)(2,1)} %constant.42.clone.perm) | copy-start | bytes 98308

commit v3 on v2

--- a/solution.py
+++ b/solution.py
@@ -123,45 +123,41 @@
 
 
 CHUNK = 18
-
-
-def work_table(groups, slots, slab_count, slab_rows):
-    table = np.zeros((5, 8, slots), np.int32)
-    table[3] = -1
+SHORTER = 9
+
+
+def work_table(groups, slots, slab_count):
+    table = np.zeros((3, 8, slots), np.int32)
+    table[1] = -1
     for octant in range(8):
         at = 0
         for place, per_octant in enumerate(groups):
             for number, shift, source in per_octant[octant]:
                 across = shift[1] * 3 + shift[2]
-                table[0, octant, at] = number
-                table[1, octant, at] = (across * 8 + source) * slab_count * slab_rows + shift[0] * slab_rows
-                table[2, octant, at] = (place * 9 + across) * 8 + source
-                table[3, octant, at] = number // 8
-                table[4, octant, at] = number % 8
+                row = (across * 8 + source) * slab_count + shift[0]
+                table[0, octant, at] = number | row << 9 | ((place * 9 + across) * 8 + source) << 18
+                table[1, octant, at] = number // 8
+                table[2, octant, at] = number % 8
                 at += 1
     return table
 
 
 def unpack_masks(packed, byte_of, shift_of):
     octants, rows, count = packed.shape
-    chunks = byte_of.shape[0]
+    lanes = byte_of.shape[1]
 
     def kernel(packed, byte_of, shift_of, out):
-        def one(octant, carry):
-            lines = lax.broadcasted_iota(jnp.int32, (count, 128), 0)
-            for c in range(chunks):
-                pick = (lines == byte_of[c, pl.ds(octant, 1), :]).astype(jnp.float32).astype(jnp.bfloat16)
-                value = jnp.dot(packed[octant], pick, preferred_element_type=jnp.float32).astype(jnp.int32)
-                bit = jnp.right_shift(value, jnp.broadcast_to(shift_of[c, pl.ds(octant, 1), :], value.shape)) & 1
-                out[c, octant] = bit.astype(jnp.float32)
-            return carry
-
-        lax.fori_loop(0, octants, one, 0)
+        lines = lax.broadcasted_iota(jnp.int32, (count, lanes), 0)
+        for octant in range(octants):
+            pick = (lines == byte_of[octant : octant + 1, :]).astype(jnp.float32).astype(jnp.bfloat16)
+            value = jnp.dot(packed[octant], pick, preferred_element_type=jnp.float32).astype(jnp.int32)
+            amount = jnp.broadcast_to(shift_of[octant : octant + 1, :], value.shape)
+            out[octant] = (jnp.right_shift(value, amount) & 1).astype(jnp.float32)
 
     vmem = pl.BlockSpec(memory_space=pltpu.VMEM)
     return pl.pallas_call(
         kernel,
-        out_shape=jax.ShapeDtypeStruct((chunks, octants, rows, 128), jnp.float32),
+        out_shape=jax.ShapeDtypeStruct((octants, rows, lanes), jnp.float32),
         in_specs=[vmem] * 3,
         out_specs=vmem,
         compiler_params=pltpu.CompilerParams(vmem_limit_bytes=16 << 20),
@@ -169,35 +165,45 @@
     )(packed, byte_of, shift_of)
 
 
-def add_terms(table, slots, first, masks, x, xp, kernels, acc):
+def add_terms(table, slots, first, slab_rows, masks, x, xp, kernels, acc):
     F = acc.shape[1] - xp.shape[1]
     rows = acc.shape[1]
 
     def masked(place, column):
-        row = pl.multiple_of(table[1, place], 16)
-        value = jnp.concatenate([x[pl.ds(row, F), :], xp[table[2, place]]], axis=0)
+        entry = table[place]
+        row = pl.multiple_of((jnp.right_shift(entry, 9) & 511) * slab_rows, 16)
+        value = jnp.concatenate([x[pl.ds(row, F), :], xp[jnp.right_shift(entry, 18)]], axis=0)
         return value * jnp.broadcast_to(column, (rows, 128)).astype(jnp.bfloat16)
 
-    def step(number, carry):
-        at = number * CHUNK
-        for octant in range(8):
-            place = octant * slots + at
-            columns = masks[first + number, octant]
-            left = jnp.concatenate([masked(place + j, columns[:, j : j + 1]) for j in range(CHUNK)], axis=1)
-            right = jnp.concatenate([kernels[table[0, place + j]] for j in range(CHUNK)], axis=0)
-            acc[octant] += jnp.dot(left, right, preferred_element_type=jnp.float32)
-        return carry
-
-    lax.fori_loop(0, slots // CHUNK, step, 0)
-
-
-def first_terms(table, slots, masks, x, xp, kernels):
-    rows = masks.shape[2]
+    longer = table[8 * slots]
+
+    def run(lead, count):
+        def one(number, carry):
+            octant = lead + number
+            columns = masks[octant]
+            for at in range(0, count, CHUNK):
+                part = range(at, min(at + CHUNK, count))
+                place = octant * slots
+                left = jnp.concatenate(
+                    [masked(place + j, columns[:, first + j : first + j + 1]) for j in part], axis=1
+                )
+                right = jnp.concatenate([kernels[table[place + j] & 511] for j in part], axis=0)
+                acc[octant] += jnp.dot(left, right, preferred_element_type=jnp.float32)
+            return carry
+
+        lax.fori_loop(0, 4, one, 0)
+
+    run(longer, slots)
+    run(4 - longer, slots - SHORTER)
+
+
+def first_terms(table, slots, slab_rows, masks, x, xp, kernels):
+    rows = masks.shape[1]
     width = kernels.shape[1]
 
     def kernel(table, masks, x, xp, kernels, acc):
         acc[...] = jnp.zeros_like(acc)
-        add_terms(table, slots, 0, masks, x, xp, kernels, acc)
+        add_terms(table, slots, 0, slab_rows, masks, x, xp, kernels, acc)
 
     vmem = pl.BlockSpec(memory_space=pltpu.VMEM)
     return pl.pallas_call(
@@ -213,35 +219,51 @@
     )(table, masks, x, xp, kernels)
 
 
-def last_terms(table, slots, first, masks, x, xp, kernels, sums, shift_ops, perm):
-    rows = masks.shape[2]
+def moved_rows(order, rows):
+    return jnp.dot(order, rows, preferred_element_type=jnp.float32).astype(jnp.bfloat16)
+
+
+def last_terms(table, slots, first, slab_rows, masks, x, xp, kernels, sums, shift_ops, perm, fine_back, parent_back):
+    rows = masks.shape[1]
     width = kernels.shape[1]
     F = perm.shape[0]
 
-    def kernel(table, masks, x, xp, kernels, sums, shift, perm, fine_out, parent_out, acc):
+    def kernel(table, masks, x, xp, kernels, sums, *refs):
+        late, (fine_out, parent_out, acc, shift, perm, fine_back, parent_back, sems) = refs[:4], refs[4:]
+        loads = []
+        for number, (source, target) in enumerate(zip(late, (shift, perm, fine_back, parent_back))):
+            load = pltpu.make_async_copy(source, target, sems.at[number])
+            load.start()
+            loads.append(load)
         acc[...] = sums[...]
-        add_terms(table, slots, first, masks, x, xp, kernels, acc)
+        add_terms(table, slots, first, slab_rows, masks, x, xp, kernels, acc)
+        for load in loads:
+            load.wait()
         far = [(acc[p, F:, :] * 0.5).astype(jnp.bfloat16) for p in range(8)]
         local = jnp.concatenate(far, axis=0)
-        parent_out[...] = local
-        ordered = jnp.dot(perm[...], local, preferred_element_type=jnp.float32).astype(jnp.bfloat16)
+        parent_out[...] = moved_rows(parent_back[...], local)
+        ordered = moved_rows(perm[...], local)
+        near = []
         for p in range(8):
             moved = jnp.dot(ordered, shift[p], preferred_element_type=jnp.float32)
-            fine_out[p] = (acc[p, :F, :] + moved).astype(jnp.bfloat16)
+            near.append((acc[p, :F, :] + moved).astype(jnp.bfloat16))
+        fine_out[...] = moved_rows(fine_back[...], jnp.concatenate(near, axis=0))
 
     vmem = pl.BlockSpec(memory_space=pltpu.VMEM)
     return pl.pallas_call(
         kernel,
         out_shape=(
-            jax.ShapeDtypeStruct((8, F, width), jnp.bfloat16),
+            jax.ShapeDtypeStruct((8 * F, width), jnp.bfloat16),
             jax.ShapeDtypeStruct((8 * (rows - F), width), jnp.bfloat16),
         ),
-        in_specs=[pl.BlockSpec(memory_space=pltpu.SMEM)] + [vmem] * 7,
+        in_specs=[pl.BlockSpec(memory_space=pltpu.SMEM)] + [vmem] * 5 + [pl.BlockSpec(memory_space=pltpu.HBM)] * 4,
         out_specs=(vmem, vmem),
-        scratch_shapes=[pltpu.VMEM((8, rows, width), jnp.float32)],
+        scratch_shapes=[pltpu.VMEM((8, rows, width), jnp.float32)]
+        + [pltpu.VMEM(v.shape, v.dtype) for v in (shift_ops, perm, fine_back, parent_back)]
+        + [pltpu.SemaphoreType.DMA((4,))],
         compiler_params=pltpu.CompilerParams(vmem_limit_bytes=16 << 20),
         name="last_terms",
-    )(table, masks, x, xp, kernels, sums, shift_ops, perm)
+    )(table, masks, x, xp, kernels, sums, shift_ops, perm, fine_back, parent_back)
 
 
 def parent_order(parent_bits):
@@ -252,6 +274,14 @@
     perm = np.zeros((count, count), np.float32)
     perm[np.arange(count), place[grid_permutation(parent_bits)]] = 1
     return perm
+
+
+def back_order(total_bits):
+    count = 2**total_bits
+    numbers = np.arange(count).reshape(-1, 8)[grid_permutation(total_bits - 3)].T.reshape(-1)
+    order = np.zeros((count, count), np.float32)
+    order[numbers, np.arange(count)] = 1
+    return order
 
 
 def on_device(fine_mult, parent_mult, fine_mask, parent_mask, kernels, shift_ops):
@@ -267,13 +297,6 @@
     G = parent_mult.shape[0] // 8
     n1, n2, n3 = fine.shape[1:4]
     m1, m2, m3 = parent.shape[1:4]
-    masks = jnp.concatenate(
-        [
-            octant_grids(fine_mask.T, fine_bits).reshape(8, F, words),
-            octant_grids(parent_mask.T, parent_bits).reshape(8, G, words),
-        ],
-        axis=1,
-    )
     is_odd = parity(0, fine_bits, device_index, device_bits)
     lists = shift_lists()
     slots = [126, 72]
@@ -282,8 +305,8 @@
         near_side, far_side = (0, 2) if odd else (2, 0)
         tables.append(
             (
-                work_table([lists[1], lists[near_side]], slots[0], n1 + 2, n2 * n3),
-                work_table([lists[far_side]], slots[1], n1 + 2, n2 * n3),
+                work_table([lists[1], lists[near_side]], slots[0], n1 + 2),
+                work_table([lists[far_side]], slots[1], n1 + 2),
             )
         )
 
@@ -293,17 +316,36 @@
     def columns(line):
         def make(pair):
             joined = np.concatenate([pair[0][line], pair[1][line]], axis=1)
-            chunked = joined.reshape(8, -1, CHUNK).transpose(1, 0, 2)
-            return np.pad(chunked, ((0, 0), (0, 0), (0, 128 - CHUNK)))
+            return np.pad(joined, ((0, 0), (0, -joined.shape[1] % 128)))
 
         return by_parity(make)
 
-    first_table = by_parity(lambda pair: pair[0][:3].reshape(3, -1))
-    last_table = by_parity(lambda pair: pair[1][:3].reshape(3, -1))
+    def entries(which):
+        def make(pair):
+            lengths = (pair[which][1] >= 0).sum(axis=1)
+            lead = 0 if lengths[0] > lengths[4] else 4
+            assert set(lengths[lead : lead + 4]) == {slots[which]}
+            assert set(lengths[4 - lead : 8 - lead]) == {slots[which] - SHORTER}
+            return np.concatenate([pair[which][0].reshape(-1), np.array([lead], np.int32)])
+
+        return by_parity(make)
+
+    first_table = entries(0)
+    last_table = entries(1)
+    fine, parent = exchange(fine, parent, 1, fine_bits, device_index, device_bits)
+    fine, parent, fine_mask, parent_mask = lax.optimization_barrier(
+        (fine, parent, fine_mask, parent_mask)
+    )
+    masks = jnp.concatenate(
+        [
+            octant_grids(fine_mask.T, fine_bits).reshape(8, F, words),
+            octant_grids(parent_mask.T, parent_bits).reshape(8, G, words),
+        ],
+        axis=1,
+    )
     packed = jnp.stack([masks & 255, jnp.right_shift(masks, 8)], axis=3).astype(jnp.bfloat16)
-    held = unpack_masks(packed.reshape(8, F + G, 2 * words), columns(3), columns(4))
-    for dim in (1, 2):
-        fine, parent = exchange(fine, parent, dim, fine_bits, device_index, device_bits)
+    held = unpack_masks(packed.reshape(8, F + G, 2 * words), columns(1), columns(2))
+    fine, parent = exchange(fine, parent, 2, fine_bits, device_index, device_bits)
     top = packed_face(fine, parent, 1, True)
     bottom = packed_face(fine, parent, 1, False)
     even_got = lax.ppermute(
@@ -340,7 +382,7 @@
     xp_even = jnp.concatenate(
         [across(parent, m2, m3), moved_parents(even_got, jnp.logical_not(is_odd))]
     ).reshape(-1, G, width)
-    sums = first_terms(first_table, slots[0], held, x_even.reshape(-1, width), xp_even, kernels)
+    sums = first_terms(first_table, slots[0], n2 * n3, held, x_even.reshape(-1, width), xp_even, kernels)
     sums, odd_got = lax.optimization_barrier((sums, odd_got))
     odd_across = across(slab(odd_got), n2, n3)
     slab_rows = n2 * n3
@@ -350,7 +392,8 @@
     fine_local, parent_local = last_terms(
         last_table,
         slots[1],
-        slots[0] // CHUNK,
+        slots[0],
+        n2 * n3,
         held,
         x_odd.reshape(-1, width),
         xp_odd,
@@ -358,22 +401,10 @@
         sums,
         shift_ops,
         jnp.asarray(parent_order(parent_bits), jnp.bfloat16),
-    )
-    fine_local = from_octants(fine_local, fine_bits)
-    parent_local = from_octants(parent_local.reshape(8, G, width), parent_bits)
+        jnp.asarray(back_order(fine_bits), jnp.bfloat16),
+        jnp.asarray(back_order(parent_bits), jnp.bfloat16),
+    )
     return fine_local, parent_local
-
-
-def from_octants(blocks, total_bits):
-    width = blocks.shape[-1]
-    bits = total_bits - 3
-    axes_order, _ = grid_order(bits)
-    grid = blocks.reshape((8,) + (2,) * bits + (width,))
-    inverse = [0] * bits
-    for position, source in enumerate(axes_order):
-        inverse[source] = position
-    moved = jnp.transpose(grid, tuple(1 + v for v in inverse) + (0, bits + 1))
-    return moved.reshape(2**total_bits, width)
 
 
 def solution(mesh):

time: 62.9 us -> 61.5 us (0.978)
  Pallas kernels: 27 us -> 24.9 us
  other arithmetic: 0.56 us -> 2.59 us
  starting transfers between devices: 21.7 us -> 23.7 us
  local copies, waits for them, and re-layouts: 9.15 us -> 7.18 us
  waiting for transfers between devices: 2.39 us -> 1.33 us
    select_n x3, other arithmetic: 0.03 us -> 2.11 us  [by_parity(): return jnp.where(is_odd, make(tables[1]), make(tables[0]))]
    ppermute x1, starting transfers between devices: 9.62 us -> 11.6 us  [on_device(): lax.ppermute(jnp.where(is_odd, top, bottom), 'box', pair_route(0, 1, fine...]
    transpose x2 -> x0, local copies, waits for them, and re-layouts: 1.64 us -> none  [from_octants(): moved = jnp.transpose(grid, tuple((1 + v for v in inverse)) + (0, bits + 1))]
    ppermute x2, waiting for transfers between devices: 2.38 us -> 1.32 us  [exchange(): lax.ppermute(odd_send, 'box', pair_route(dim, 1, low_bits, device_bits))]
    pallas_call x2, Pallas kernels: 12 us -> 10.9 us  [the longest x1 10.6 us: last_terms(): pl.pallas_call(kernel, out_shape=(jax.ShapeDtypeStruct((8 * F, width), jn...]
    pallas_call x1, Pallas kernels: 15 us -> 14 us  [first_terms(): pl.pallas_call(kernel, out_shape=jax.ShapeDtypeStruct((8, rows, width), j...]
    unnamed x71 -> x59, local copies, waits for them, and re-layouts: 3.82 us -> 3.18 us
  transfers between devices with their start and end apart: 6 -> 6, of which waited for: 1 -> 2; matrix products, arithmetic and copies ran while one was open for 6% -> 8% of each run, Pallas kernels for 29% -> 23%
where the time goes in v3:
time: 61.5 us; the launch traced here: 61.1 us
  Pallas kernels  24.9 us (40%)
  starting transfers between devices  23.7 us (39%)
  local copies, waits for them, and re-layouts  7.18 us (12%)
  other arithmetic  2.59 us (4%)
  between operations  1.37 us (2%)
  waiting for transfers between devices  1.33 us (2%)
    pallas_call x1, Pallas kernels, first_terms(): pl.pallas_call(kernel, out_shape=jax.ShapeDtypeStruct((8, rows, width), j...  14 us
    ppermute x1, starting transfers between devices, on_device(): lax.ppermute(jnp.where(is_odd, top, bottom), 'box', pair_route(0, 1, fine...  11.6 us
    pallas_call x1, Pallas kernels, last_terms(): pl.pallas_call(kernel, out_shape=(jax.ShapeDtypeStruct((8 * F, width), jn...  10.6 us
    ppermute x2, starting transfers between devices, exchange(): lax.ppermute(odd_send, 'box', pair_route(dim, 1, low_bits, device_bits))  10.1 us
    unnamed x59, local copies, waits for them, and re-layouts  3.18 us
    select_n x3, other arithmetic, by_parity(): return jnp.where(is_odd, make(tables[1]), make(tables[0]))  2.11 us
    ppermute x2, starting transfers between devices, exchange(): lax.ppermute(even_send, 'box', pair_route(dim, 0, low_bits, device_bits))  1.97 us
    transpose x4, local copies, waits for them, and re-layouts, to_grid(): jnp.transpose(bitwise, tuple(axes_order) + extra)  1.84 us
  transfers between devices with their start and end apart: 6, of which 2 were waited for; matrix products, arithmetic and copies ran while one was open for 8% of the time, Pallas kernels for 23%

profile of v3, /device:TPU:31, one launch (start us, length us, event | category | flops | bytes accessed | tf_op | source)
XLA Modules:
  0.0 61.1 jit_solution(17106073905075531653)
XLA Ops:
  0.7 1.0 %copy.139 = bf16[2,2,2,2,2,2,2,8,128]{8,7,6,5,4,3,2,1,0:T(8,128)(2,1)S(1)} copy(bf16[2,2,2,2,2,2,2,8,128]{8,7,6,3,1,5,2,0,4:T(8,128)(2,1)} %bitcast.157) | data formatting | bytes 524288 | tf_op jit(solution)/shard_map/transpose | solution.py:41
  1.7 0.8 %copy.140 = bf16[2,2,2,2,8,128]{5,4,3,2,1,0:T(8,128)(2,1)S(1)} copy(bf16[2,2,2,2,8,128]{5,4,3,1,0,2:T(8,128)(2,1)} %bitcast.203) | data formatting | bytes 65536 | tf_op jit(solution)/shard_map/transpose | solution.py:41
  2.5 0.8 %collective-permute-start = (bf16[8,40,128]{2,0,1:T(8,128)(2,1)S(1)}, bf16[8,40,128]{2,0,1:T(8,128)(2,1)S(1)}, u32[]{:S(2)}, u32[]{:S(2)}) collective-permute-start(bf16[8,40,128]{2,0,1:T(8,128)(2,1)S(1)} %get-tuple-element.35), channel_id=1, source_target_pairs={{0,1},{1,0},{2,3},{3,2},{4,5},{5,4},{6,7},{7,6},{8,9},{9,8},{10,11... | collective-permute-start | bytes 245768 | tf_op jit(solution)/shard_map/ppermute | solution.py:97
  3.2 5.0 %collective-permute-start.1 = (bf16[8,40,128]{2,0,1:T(8,128)(2,1)S(1)}, bf16[8,40,128]{2,0,1:T(8,128)(2,1)S(1)}, u32[]{:S(2)}, u32[]{:S(2)}) collective-permute-start(bf16[8,40,128]{2,0,1:T(8,128)(2,1)S(1)} %get-tuple-element.36), channel_id=1, source_target_pairs={{1,8},{3,10},{5,12},{7,14},{8,1},{9,64},{10,3},{11,66},{12,5},{13,... | collective-permute-start | bytes 245768 | tf_op jit(solution)/shard_map/ppermute | solution.py:96
  8.2 0.7 %broadcast_select_fusion.12.table = s32[1009]{0:T(1024)S(1)} fusion(s32[1009]{0:T(1024)} %constant.38.clone, s32[1009]{0:T(1024)} %constant.39.clone, pred[]{:T(512)S(6)} %eq.9), kind=kLoop, calls=%fused_computation.94 | loop fusion | flops 1009 | bytes 12109 | tf_op jit(solution)/shard_map/jit(_where)/select_n | solution.py:314
  8.9 0.7 %broadcast_select_fusion.10 = (s32[8,256]{1,0:T(8,128)S(1)}, s32[8,256]{1,0:T(8,128)S(1)}) fusion(s32[8,256]{1,0:T(8,128)} %constant.44.clone, s32[8,256]{1,0:T(8,128)} %constant.45.clone, pred[]{:T(512)S(6)} %eq.9, s32[8,256]{1,0:T(8,128)} %constant.42.clone, s32[8,256]{1,0:T(8,128)} %constant.43.clone), kind=kLoop, calls=%fused_computation.92 | loop fusion | flops 4096 | bytes 49153 | tf_op jit(solution)/shard_map/jit(_where)/select_n | solution.py:314
  9.7 0.7 %broadcast_select_fusion.13.table = s32[577]{0:T(1024)S(1)} fusion(s32[577]{0:T(1024)} %constant.40.clone, s32[577]{0:T(1024)} %constant.41.clone, pred[]{:T(512)S(6)} %eq.9), kind=kLoop, calls=%fused_computation.95 | loop fusion | flops 577 | bytes 6925 | tf_op jit(solution)/shard_map/jit(_where)/select_n | solution.py:314
  10.3 0.4 collective-permute-done.1
  11.0 1.2 %collective-permute-start.2 = (bf16[8,32,128]{2,0,1:T(8,128)(2,1)S(1)}, bf16[8,32,128]{2,0,1:T(8,128)(2,1)S(1)}, u32[]{:S(2)}, u32[]{:S(2)}) collective-permute-start(bf16[8,32,128]{2,0,1:T(8,128)(2,1)S(1)} %get-tuple-element.39), channel_id=1, source_target_pairs={{0,4},{1,5},{2,6},{3,7},{4,0},{5,1},{6,2},{7,3},{8,12},{9,13},{10,... | collective-permute-start | bytes 196616 | tf_op jit(solution)/shard_map/ppermute | solution.py:97
  12.2 5.1 %collective-permute-start.3 = (bf16[8,32,128]{2,0,1:T(8,128)(2,1)S(1)}, bf16[8,32,128]{2,0,1:T(8,128)(2,1)S(1)}, u32[]{:S(2)}, u32[]{:S(2)}) collective-permute-start(bf16[8,32,128]{2,0,1:T(8,128)(2,1)S(1)} %get-tuple-element.40), channel_id=1, source_target_pairs={{4,32},{5,33},{6,34},{7,35},{12,40},{13,41},{14,42},{15,43},{20,48... | collective-permute-start | bytes 196616 | tf_op jit(solution)/shard_map/ppermute | solution.py:96
  17.3 0.2 copy.141
  17.6 0.2 copy.146
  17.9 0.1 copy.144
  18.0 0.1 copy.147
  18.2 0.2 copy.148.packed
  18.4 0.3 unpack.1.masks
  18.8 0.9 %collective-permute-done.3 = bf16[8,32,128]{2,0,1:T(8,128)(2,1)S(1)} collective-permute-done((bf16[8,32,128]{2,0,1:T(8,128)(2,1)S(1)}, bf16[8,32,128]{2,0,1:T(8,128)(2,1)S(1)}, u32[]{:S(2)}, u32[]{:S(2)}) %collective-permute-start.3) | collective-permute-done | bytes 65568 | tf_op jit(solution)/shard_map/ppermute | solution.py:96
  20.0 11.6 %collective-permute-start.5 = (bf16[8,84,128]{2,0,1:T(8,128)(2,1)S(1)}, bf16[8,84,128]{2,0,1:T(8,128)(2,1)S(1)}, u32[]{:S(2)}, u32[]{:S(2)}) collective-permute-start(bf16[8,84,128]{2,0,1:T(8,128)(2,1)S(1)} %get-tuple-element.27), channel_id=1, source_target_pairs={{2,16},{3,17},{6,20},{7,21},{10,24},{11,25},{14,28},{15,29},{16,2}... | collective-permute-start | bytes 516104 | tf_op jit(solution)/shard_map/ppermute | solution.py:354
  31.9 0.1 pad_maximum_fusion
  32.0 0.7 %fusion.6 = (bf16[8,6,4,8,128]{4,0,3,2,1:T(8,128)(2,1)S(1)}, bf16[8,6,4,8,128]{4,0,3,2,1:T(8,128)(2,1)S(1)}, bf16[8,6,4,8,128]{4,0,3,2,1:T(8,128)(2,1)S(1)}, bf1...) fusion(bf16[8,6,6,10,128]{4,0,3,2,1:T(8,128)(2,1)S(1)} %pad_max, ...), kind=kLoop, calls=%fused_computation.98 | loop fusion | bytes 7077888 | tf_op jit(solution)/shard_map/slice | solution.py:368
  33.0 0.1 copy_dynamic-update-slice_fusion.6
  33.1 0.1 copy_dynamic-update-slice_fusion.5
  33.2 0.1 copy_dynamic-update-slice_fusion.4
  33.3 0.1 copy_dynamic-update-slice_fusion.3
  33.4 0.1 copy_dynamic-update-slice_fusion.2
  33.5 0.1 copy_dynamic-update-slice_fusion.1
  33.6 0.1 copy_dynamic-update-slice_fusion
  33.8 0.3 slice-done.1
  34.1 0.8 %slice-done.2 = s8[1966080]{0:T(1024)(128)(4,1)S(1)} async-done(((s8[10354688]{0:T(1024)(128)(4,1)}), s8[1966080]{0:T(1024)(128)(4,1)S(1)}, s32[]{:S(2)}) %slice-start.2) | async-done | bytes 1966104
  34.9 14.0 %first_terms.1.sums = f32[8,144,128]{2,1,0:T(8,128)S(1)} custom-call(s32[1009]{0:T(1024)S(1)} %broadcast_select_fusion.12.table, f32[8,144,256]{2,1,0:T(8,128)S(1)} %unpack.1.masks, bf16[13824,128]{1,0:T(8,128)(2,1)S(1)} %bitcast.116, bf16[144,16,128]{2,1,0:T(8,128)(2,1)S(1)} %bitcast.119, bf16[316,128,128]{2,1,0:T(8,128)(2,1)S(1)} %bitcast.115), custom_call_target="tpu_custom_call" | custom-call | flops 4756340736 | bytes 3538944 | tf_op jit(solution)/shard_map/first_terms/pallas_call | solution.py:209
  49.7 0.8 %copy-done = bf16[1024,1024]{1,0:T(8,128)(2,1)S(1)} copy-done((bf16[1024,1024]{1,0:T(8,128)(2,1)S(1)}, bf16[1024,1024]{1,0:T(8,128)(2,1)}, u32[]{:S(2)}) %copy-start) | copy-done | bytes 2097176
  50.5 10.6 %last_terms.1 = (bf16[1024,128]{1,0:T(8,128)(2,1)}, bf16[128,128]{1,0:T(8,128)(2,1)}) custom-call(s32[577]{0:T(1024)S(1)} %broadcast_select_fusion.13.table, f32[8,144,256]{2,1,0:T(8,128)S(1)} %unpack.1.masks, bf16[13824,128]{1,0:T(8,128)(2,1)S(1)} %bitcast.117, bf16[72,16,128]{2,1,0:T(8,128)(2,1)S(1)} %bitcast.118, bf16[316,128,128]{2,1,0:T(8,128)(2,1)S(1)} %bitcast.115, ...), custom_call_target="tpu_custom_call" | custom-call | tf_op jit(solution)/shard_map/last_terms/pallas_call | solution.py:253
  (97 shorter events, 1.7 us)
Async XLA Ops:
  0.6 16.7 %copy-start.4 = (s32[20,1024]{1,0:T(8,128)S(1)}, s32[20,1024]{1,0:T(8,128)}, u32[]{:S(2)}) copy-start(s32[20,1024]{1,0:T(8,128)} %param.19) | copy-start | bytes 245764
  0.6 17.2 %copy-start.5 = (s32[20,128]{1,0:T(8,128)S(1)}, s32[20,128]{1,0:T(8,128)}, u32[]{:S(2)}) copy-start(s32[20,128]{1,0:T(8,128)} %param.20) | copy-start | bytes 30724
  2.5 7.9 %collective-permute-start = (bf16[8,40,128]{2,0,1:T(8,128)(2,1)S(1)}, bf16[8,40,128]{2,0,1:T(8,128)(2,1)S(1)}, u32[]{:S(2)}, u32[]{:S(2)}) collective-permute-start(bf16[8,40,128]{2,0,1:T(8,128)(2,1)S(1)} %get-tuple-element.35), channel_id=1, source_target_pairs={{0,1},{1,0},{2,3},{3,2},{4,5},{5,4},{6,7},{7,6},{8,9},{9,8},{10,11... | collective-permute-start | bytes 245768 | tf_op jit(solution)/shard_map/ppermute | solution.py:97
  3.2 7.5 %collective-permute-start.1 = (bf16[8,40,128]{2,0,1:T(8,128)(2,1)S(1)}, bf16[8,40,128]{2,0,1:T(8,128)(2,1)S(1)}, u32[]{:S(2)}, u32[]{:S(2)}) collective-permute-start(bf16[8,40,128]{2,0,1:T(8,128)(2,1)S(1)} %get-tuple-element.36), channel_id=1, source_target_pairs={{1,8},{3,10},{5,12},{7,14},{8,1},{9,64},{10,3},{11,66},{12,5},{13,... | collective-permute-start | bytes 245768 | tf_op jit(solution)/shard_map/ppermute | solution.py:96
  11.0 7.8 %collective-permute-start.2 = (bf16[8,32,128]{2,0,1:T(8,128)(2,1)S(1)}, bf16[8,32,128]{2,0,1:T(8,128)(2,1)S(1)}, u32[]{:S(2)}, u32[]{:S(2)}) collective-permute-start(bf16[8,32,128]{2,0,1:T(8,128)(2,1)S(1)} %get-tuple-element.39), channel_id=1, source_target_pairs={{0,4},{1,5},{2,6},{3,7},{4,0},{5,1},{6,2},{7,3},{8,12},{9,13},{10,... | collective-permute-start | bytes 196616 | tf_op jit(solution)/shard_map/ppermute | solution.py:97
  12.2 7.5 %collective-permute-start.3 = (bf16[8,32,128]{2,0,1:T(8,128)(2,1)S(1)}, bf16[8,32,128]{2,0,1:T(8,128)(2,1)S(1)}, u32[]{:S(2)}, u32[]{:S(2)}) collective-permute-start(bf16[8,32,128]{2,0,1:T(8,128)(2,1)S(1)} %get-tuple-element.40), channel_id=1, source_target_pairs={{4,32},{5,33},{6,34},{7,35},{12,40},{13,41},{14,42},{15,43},{20,48... | collective-permute-start | bytes 196616 | tf_op jit(solution)/shard_map/ppermute | solution.py:96
  18.4 15.3 %slice-start = ((s8[10354688]{0:T(1024)(128)(4,1)}), s8[4194304]{0:T(1024)(128)(4,1)S(1)}, s32[]{:S(2)}) async-start(s8[10354688]{0:T(1024)(128)(4,1)} %bitcast.114), calls=%async_computation | async-start | bytes 8388608
  19.9 11.8 %collective-permute-start.4 = (bf16[8,84,128]{2,0,1:T(8,128)(2,1)S(1)}, bf16[8,84,128]{2,0,1:T(8,128)(2,1)S(1)}, u32[]{:S(2)}, u32[]{:S(2)}) collective-permute-start(bf16[8,84,128]{2,0,1:T(8,128)(2,1)S(1)} %get-tuple-element.28), channel_id=1, source_target_pairs={{0,2},{1,3},{2,0},{3,1},{4,6},{5,7},{6,4},{7,5},{8,10},{9,11},{10,... | collective-permute-start | bytes 516104 | tf_op jit(solution)/shard_map/ppermute | solution.py:351
  20.0 28.9 %collective-permute-start.5 = (bf16[8,84,128]{2,0,1:T(8,128)(2,1)S(1)}, bf16[8,84,128]{2,0,1:T(8,128)(2,1)S(1)}, u32[]{:S(2)}, u32[]{:S(2)}) collective-permute-start(bf16[8,84,128]{2,0,1:T(8,128)(2,1)S(1)} %get-tuple-element.27), channel_id=1, source_target_pairs={{2,16},{3,17},{6,20},{7,21},{10,24},{11,25},{14,28},{15,29},{16,2}... | collective-permute-start | bytes 516104 | tf_op jit(solution)/shard_map/ppermute | solution.py:354
  31.9 2.2 %slice-start.1 = ((s8[10354688]{0:T(1024)(128)(4,1)}), s8[4194304]{0:T(1024)(128)(4,1)S(1)}, s32[]{:S(2)}) async-start(s8[10354688]{0:T(1024)(128)(4,1)} %bitcast.114), calls=%async_computation.1 | async-start | bytes 8388608
  32.7 2.2 %slice-start.2 = ((s8[10354688]{0:T(1024)(128)(4,1)}), s8[1966080]{0:T(1024)(128)(4,1)S(1)}, s32[]{:S(2)}) async-start(s8[10354688]{0:T(1024)(128)(4,1)} %bitcast.114), calls=%async_computation.2 | async-start | bytes 3932160
  48.9 1.6 %copy-start = (bf16[1024,1024]{1,0:T(8,128)(2,1)S(1)}, bf16[1024,1024]{1,0:T(8,128)(2,1)}, u32[]{:S(2)}) copy-start(bf16[1024,1024]{1,0:T(8,128)(2,1)} %constant.47.clone.refs_2_) | copy-start | bytes 6291460
  48.9 1.6 %copy-start.1 = (bf16[8,128,128]{2,1,0:T(8,128)(2,1)S(1)}, bf16[8,128,128]{2,1,0:T(8,128)(2,1)}, u32[]{:S(2)}) copy-start(bf16[8,128,128]{2,1,0:T(8,128)(2,1)} %refs_0_.1) | copy-start | bytes 786436
  48.9 1.6 %copy-start.2 = (bf16[128,128]{1,0:T(8,128)(2,1)S(1)}, bf16[128,128]{1,0:T(8,128)(2,1)}, u32[]{:S(2)}) copy-start(bf16[128,128]{1,0:T(8,128)(2,1)} %constant.46.clone.refs_1_) | copy-start | bytes 98308
  49.0 1.6 %copy-start.3 = (bf16[128,128]{1,0:T(8,128)(2,1)S(1)}, bf16[128,128]{1,0:T(8,128)(2,1)}, u32[]{:S(2)}) copy-start(bf16[128,128]{1,0:T(8,128)(2,1)} %constant.48.clone.refs_3_) | copy-start | bytes 98308

commit v4 on v3

--- a/solution.py
+++ b/solution.py
@@ -228,17 +228,11 @@
     width = kernels.shape[1]
     F = perm.shape[0]
 
-    def kernel(table, masks, x, xp, kernels, sums, *refs):
-        late, (fine_out, parent_out, acc, shift, perm, fine_back, parent_back, sems) = refs[:4], refs[4:]
-        loads = []
-        for number, (source, target) in enumerate(zip(late, (shift, perm, fine_back, parent_back))):
-            load = pltpu.make_async_copy(source, target, sems.at[number])
-            load.start()
-            loads.append(load)
+    def kernel(
+        table, masks, x, xp, kernels, sums, shift, perm, fine_back, parent_back, fine_out, parent_out, acc, rows_out
+    ):
         acc[...] = sums[...]
         add_terms(table, slots, first, slab_rows, masks, x, xp, kernels, acc)
-        for load in loads:
-            load.wait()
         far = [(acc[p, F:, :] * 0.5).astype(jnp.bfloat16) for p in range(8)]
         local = jnp.concatenate(far, axis=0)
         parent_out[...] = moved_rows(parent_back[...], local)
@@ -247,7 +241,10 @@
         for p in range(8):
             moved = jnp.dot(ordered, shift[p], preferred_element_type=jnp.float32)
             near.append((acc[p, :F, :] + moved).astype(jnp.bfloat16))
-        fine_out[...] = moved_rows(fine_back[...], jnp.concatenate(near, axis=0))
+        whole = jnp.dot(fine_back[...], jnp.concatenate(near, axis=1), preferred_element_type=jnp.float32)
+        for p in range(8):
+            rows_out[:, p, :] = whole[:, p * width : (p + 1) * width]
+        fine_out[...] = rows_out[...].reshape(8 * F, width).astype(jnp.bfloat16)
 
     vmem = pl.BlockSpec(memory_space=pltpu.VMEM)
     return pl.pallas_call(
@@ -256,11 +253,9 @@
             jax.ShapeDtypeStruct((8 * F, width), jnp.bfloat16),
             jax.ShapeDtypeStruct((8 * (rows - F), width), jnp.bfloat16),
         ),
-        in_specs=[pl.BlockSpec(memory_space=pltpu.SMEM)] + [vmem] * 5 + [pl.BlockSpec(memory_space=pltpu.HBM)] * 4,
+        in_specs=[pl.BlockSpec(memory_space=pltpu.SMEM)] + [vmem] * 9,
         out_specs=(vmem, vmem),
-        scratch_shapes=[pltpu.VMEM((8, rows, width), jnp.float32)]
-        + [pltpu.VMEM(v.shape, v.dtype) for v in (shift_ops, perm, fine_back, parent_back)]
-        + [pltpu.SemaphoreType.DMA((4,))],
+        scratch_shapes=[pltpu.VMEM((8, rows, width), jnp.float32), pltpu.VMEM((F, 8, width), jnp.float32)],
         compiler_params=pltpu.CompilerParams(vmem_limit_bytes=16 << 20),
         name="last_terms",
     )(table, masks, x, xp, kernels, sums, shift_ops, perm, fine_back, parent_back)
@@ -274,6 +269,12 @@
     perm = np.zeros((count, count), np.float32)
     perm[np.arange(count), place[grid_permutation(parent_bits)]] = 1
     return perm
+
+
+def grid_back(total_bits):
+    order = np.zeros((2**total_bits, 2**total_bits), np.float32)
+    order[grid_permutation(total_bits), np.arange(2**total_bits)] = 1
+    return order
 
 
 def back_order(total_bits):
@@ -401,7 +402,7 @@
         sums,
         shift_ops,
         jnp.asarray(parent_order(parent_bits), jnp.bfloat16),
-        jnp.asarray(back_order(fine_bits), jnp.bfloat16),
+        jnp.asarray(grid_back(parent_bits), jnp.bfloat16),
         jnp.asarray(back_order(parent_bits), jnp.bfloat16),
     )
     return fine_local, parent_local

time: 61.5 us -> 60.3 us (0.980)
  local copies, waits for them, and re-layouts: 7.18 us -> 6.54 us
    unnamed x59, local copies, waits for them, and re-layouts: 3.18 us -> 2.53 us
  transfers between devices with their start and end apart: 6 -> 6, of which waited for: 2 -> 2; matrix products, arithmetic and copies ran while one was open for 8% -> 8% of each run, Pallas kernels for 23% -> 24%
where the time goes in v4:
time: 60.3 us; the launch traced here: 59.9 us
  Pallas kernels  24.4 us (40%)
  starting transfers between devices  23.7 us (39%)
  local copies, waits for them, and re-layouts  6.54 us (11%)
  other arithmetic  2.59 us (4%)
  between operations  1.37 us (2%)
  waiting for transfers between devices  1.33 us (2%)
    pallas_call x1, Pallas kernels, first_terms(): pl.pallas_call(kernel, out_shape=jax.ShapeDtypeStruct((8, rows, width), j...  14 us
    ppermute x1, starting transfers between devices, on_device(): lax.ppermute(jnp.where(is_odd, top, bottom), 'box', pair_route(0, 1, fine...  11.6 us
    ppermute x2, starting transfers between devices, exchange(): lax.ppermute(odd_send, 'box', pair_route(dim, 1, low_bits, device_bits))  10.1 us
    pallas_call x1, Pallas kernels, last_terms(): pl.pallas_call(kernel, out_shape=(jax.ShapeDtypeStruct((8 * F, width), jn...  10 us
    unnamed x59, local copies, waits for them, and re-layouts  2.53 us
    select_n x3, other arithmetic, by_parity(): return jnp.where(is_odd, make(tables[1]), make(tables[0]))  2.11 us
    ppermute x2, starting transfers between devices, exchange(): lax.ppermute(even_send, 'box', pair_route(dim, 0, low_bits, device_bits))  1.97 us
    transpose x4, local copies, waits for them, and re-layouts, to_grid(): jnp.transpose(bitwise, tuple(axes_order) + extra)  1.84 us
  transfers between devices with their start and end apart: 6, of which 2 were waited for; matrix products, arithmetic and copies ran while one was open for 8% of the time, Pallas kernels for 24%

profile of v4, /device:TPU:31, one launch (start us, length us, event | category | flops | bytes accessed | tf_op | source)
XLA Modules:
  0.0 59.9 jit_solution(9102140434833264675)
XLA Ops:
  0.7 1.0 %copy.139 = bf16[2,2,2,2,2,2,2,8,128]{8,7,6,5,4,3,2,1,0:T(8,128)(2,1)S(1)} copy(bf16[2,2,2,2,2,2,2,8,128]{8,7,6,3,1,5,2,0,4:T(8,128)(2,1)} %bitcast.157) | data formatting | bytes 524288 | tf_op jit(solution)/shard_map/transpose | solution.py:41
  1.7 0.8 %copy.140 = bf16[2,2,2,2,8,128]{5,4,3,2,1,0:T(8,128)(2,1)S(1)} copy(bf16[2,2,2,2,8,128]{5,4,3,1,0,2:T(8,128)(2,1)} %bitcast.203) | data formatting | bytes 65536 | tf_op jit(solution)/shard_map/transpose | solution.py:41
  2.5 0.8 %collective-permute-start = (bf16[8,40,128]{2,0,1:T(8,128)(2,1)S(1)}, bf16[8,40,128]{2,0,1:T(8,128)(2,1)S(1)}, u32[]{:S(2)}, u32[]{:S(2)}) collective-permute-start(bf16[8,40,128]{2,0,1:T(8,128)(2,1)S(1)} %get-tuple-element.35), channel_id=1, source_target_pairs={{0,1},{1,0},{2,3},{3,2},{4,5},{5,4},{6,7},{7,6},{8,9},{9,8},{10,11... | collective-permute-start | bytes 245768 | tf_op jit(solution)/shard_map/ppermute | solution.py:97
  3.2 5.0 %collective-permute-start.1 = (bf16[8,40,128]{2,0,1:T(8,128)(2,1)S(1)}, bf16[8,40,128]{2,0,1:T(8,128)(2,1)S(1)}, u32[]{:S(2)}, u32[]{:S(2)}) collective-permute-start(bf16[8,40,128]{2,0,1:T(8,128)(2,1)S(1)} %get-tuple-element.36), channel_id=1, source_target_pairs={{1,8},{3,10},{5,12},{7,14},{8,1},{9,64},{10,3},{11,66},{12,5},{13,... | collective-permute-start | bytes 245768 | tf_op jit(solution)/shard_map/ppermute | solution.py:96
  8.2 0.7 %broadcast_select_fusion.12.table = s32[1009]{0:T(1024)S(1)} fusion(s32[1009]{0:T(1024)} %constant.38.clone, s32[1009]{0:T(1024)} %constant.39.clone, pred[]{:T(512)S(6)} %eq.9), kind=kLoop, calls=%fused_computation.94 | loop fusion | flops 1009 | bytes 12109 | tf_op jit(solution)/shard_map/jit(_where)/select_n | solution.py:315
  8.9 0.7 %broadcast_select_fusion.10 = (s32[8,256]{1,0:T(8,128)S(1)}, s32[8,256]{1,0:T(8,128)S(1)}) fusion(s32[8,256]{1,0:T(8,128)} %constant.44.clone, s32[8,256]{1,0:T(8,128)} %constant.45.clone, pred[]{:T(512)S(6)} %eq.9, s32[8,256]{1,0:T(8,128)} %constant.42.clone, s32[8,256]{1,0:T(8,128)} %constant.43.clone), kind=kLoop, calls=%fused_computation.92 | loop fusion | flops 4096 | bytes 49153 | tf_op jit(solution)/shard_map/jit(_where)/select_n | solution.py:315
  9.7 0.7 %broadcast_select_fusion.13.table = s32[577]{0:T(1024)S(1)} fusion(s32[577]{0:T(1024)} %constant.40.clone, s32[577]{0:T(1024)} %constant.41.clone, pred[]{:T(512)S(6)} %eq.9), kind=kLoop, calls=%fused_computation.95 | loop fusion | flops 577 | bytes 6925 | tf_op jit(solution)/shard_map/jit(_where)/select_n | solution.py:315
  10.3 0.4 collective-permute-done.1
  11.0 1.2 %collective-permute-start.2 = (bf16[8,32,128]{2,0,1:T(8,128)(2,1)S(1)}, bf16[8,32,128]{2,0,1:T(8,128)(2,1)S(1)}, u32[]{:S(2)}, u32[]{:S(2)}) collective-permute-start(bf16[8,32,128]{2,0,1:T(8,128)(2,1)S(1)} %get-tuple-element.39), channel_id=1, source_target_pairs={{0,4},{1,5},{2,6},{3,7},{4,0},{5,1},{6,2},{7,3},{8,12},{9,13},{10,... | collective-permute-start | bytes 196616 | tf_op jit(solution)/shard_map/ppermute | solution.py:97
  12.2 5.1 %collective-permute-start.3 = (bf16[8,32,128]{2,0,1:T(8,128)(2,1)S(1)}, bf16[8,32,128]{2,0,1:T(8,128)(2,1)S(1)}, u32[]{:S(2)}, u32[]{:S(2)}) collective-permute-start(bf16[8,32,128]{2,0,1:T(8,128)(2,1)S(1)} %get-tuple-element.40), channel_id=1, source_target_pairs={{4,32},{5,33},{6,34},{7,35},{12,40},{13,41},{14,42},{15,43},{20,48... | collective-permute-start | bytes 196616 | tf_op jit(solution)/shard_map/ppermute | solution.py:96
  17.3 0.2 copy.141
  17.6 0.2 copy.146
  17.9 0.1 copy.144
  18.0 0.1 copy.147
  18.2 0.2 copy.148.packed
  18.4 0.3 unpack.1.masks
  18.8 0.9 %collective-permute-done.3 = bf16[8,32,128]{2,0,1:T(8,128)(2,1)S(1)} collective-permute-done((bf16[8,32,128]{2,0,1:T(8,128)(2,1)S(1)}, bf16[8,32,128]{2,0,1:T(8,128)(2,1)S(1)}, u32[]{:S(2)}, u32[]{:S(2)}) %collective-permute-start.3) | collective-permute-done | bytes 65568 | tf_op jit(solution)/shard_map/ppermute | solution.py:96
  20.0 11.6 %collective-permute-start.5 = (bf16[8,84,128]{2,0,1:T(8,128)(2,1)S(1)}, bf16[8,84,128]{2,0,1:T(8,128)(2,1)S(1)}, u32[]{:S(2)}, u32[]{:S(2)}) collective-permute-start(bf16[8,84,128]{2,0,1:T(8,128)(2,1)S(1)} %get-tuple-element.27), channel_id=1, source_target_pairs={{2,16},{3,17},{6,20},{7,21},{10,24},{11,25},{14,28},{15,29},{16,2}... | collective-permute-start | bytes 516104 | tf_op jit(solution)/shard_map/ppermute | solution.py:355
  31.9 0.1 pad_maximum_fusion
  32.0 0.7 %fusion.6 = (bf16[8,6,4,8,128]{4,0,3,2,1:T(8,128)(2,1)S(1)}, bf16[8,6,4,8,128]{4,0,3,2,1:T(8,128)(2,1)S(1)}, bf16[8,6,4,8,128]{4,0,3,2,1:T(8,128)(2,1)S(1)}, bf1...) fusion(bf16[8,6,6,10,128]{4,0,3,2,1:T(8,128)(2,1)S(1)} %pad_max, ...), kind=kLoop, calls=%fused_computation.98 | loop fusion | bytes 7077888 | tf_op jit(solution)/shard_map/slice | solution.py:369
  33.0 0.1 copy_dynamic-update-slice_fusion.6
  33.1 0.1 copy_dynamic-update-slice_fusion.5
  33.2 0.1 copy_dynamic-update-slice_fusion.4
  33.3 0.1 copy_dynamic-update-slice_fusion.3
  33.4 0.1 copy_dynamic-update-slice_fusion.2
  33.5 0.1 copy_dynamic-update-slice_fusion.1
  33.6 0.1 copy_dynamic-update-slice_fusion
  33.8 0.3 slice-done.1
  34.1 0.8 %slice-done.2 = s8[1966080]{0:T(1024)(128)(4,1)S(1)} async-done(((s8[10354688]{0:T(1024)(128)(4,1)}), s8[1966080]{0:T(1024)(128)(4,1)S(1)}, s32[]{:S(2)}) %slice-start.2) | async-done | bytes 1966104
  34.9 14.0 %first_terms.1.sums = f32[8,144,128]{2,1,0:T(8,128)S(1)} custom-call(s32[1009]{0:T(1024)S(1)} %broadcast_select_fusion.12.table, f32[8,144,256]{2,1,0:T(8,128)S(1)} %unpack.1.masks, bf16[13824,128]{1,0:T(8,128)(2,1)S(1)} %bitcast.116, bf16[144,16,128]{2,1,0:T(8,128)(2,1)S(1)} %bitcast.119, bf16[316,128,128]{2,1,0:T(8,128)(2,1)S(1)} %bitcast.115), custom_call_target="tpu_custom_call" | custom-call | flops 4756340736 | bytes 3538944 | tf_op jit(solution)/shard_map/first_terms/pallas_call | solution.py:209
  49.7 0.1 copy-done
  49.9 10.0 %last_terms.1 = (bf16[1024,128]{1,0:T(8,128)(2,1)}, bf16[128,128]{1,0:T(8,128)(2,1)}) custom-call(s32[577]{0:T(1024)S(1)} %broadcast_select_fusion.13.table, f32[8,144,256]{2,1,0:T(8,128)S(1)} %unpack.1.masks, bf16[13824,128]{1,0:T(8,128)(2,1)S(1)} %bitcast.117, bf16[72,16,128]{2,1,0:T(8,128)(2,1)S(1)} %bitcast.118, bf16[316,128,128]{2,1,0:T(8,128)(2,1)S(1)} %bitcast.115, ...), custom_call_target="tpu_custom_call" | custom-call | tf_op jit(solution)/shard_map/last_terms/pallas_call | solution.py:250
  (97 shorter events, 1.7 us)
Async XLA Ops:
  0.6 16.7 %copy-start.4 = (s32[20,1024]{1,0:T(8,128)S(1)}, s32[20,1024]{1,0:T(8,128)}, u32[]{:S(2)}) copy-start(s32[20,1024]{1,0:T(8,128)} %param.19) | copy-start | bytes 245764
  0.6 17.2 %copy-start.5 = (s32[20,128]{1,0:T(8,128)S(1)}, s32[20,128]{1,0:T(8,128)}, u32[]{:S(2)}) copy-start(s32[20,128]{1,0:T(8,128)} %param.20) | copy-start | bytes 30724
  2.5 7.9 %collective-permute-start = (bf16[8,40,128]{2,0,1:T(8,128)(2,1)S(1)}, bf16[8,40,128]{2,0,1:T(8,128)(2,1)S(1)}, u32[]{:S(2)}, u32[]{:S(2)}) collective-permute-start(bf16[8,40,128]{2,0,1:T(8,128)(2,1)S(1)} %get-tuple-element.35), channel_id=1, source_target_pairs={{0,1},{1,0},{2,3},{3,2},{4,5},{5,4},{6,7},{7,6},{8,9},{9,8},{10,11... | collective-permute-start | bytes 245768 | tf_op jit(solution)/shard_map/ppermute | solution.py:97
  3.2 7.5 %collective-permute-start.1 = (bf16[8,40,128]{2,0,1:T(8,128)(2,1)S(1)}, bf16[8,40,128]{2,0,1:T(8,128)(2,1)S(1)}, u32[]{:S(2)}, u32[]{:S(2)}) collective-permute-start(bf16[8,40,128]{2,0,1:T(8,128)(2,1)S(1)} %get-tuple-element.36), channel_id=1, source_target_pairs={{1,8},{3,10},{5,12},{7,14},{8,1},{9,64},{10,3},{11,66},{12,5},{13,... | collective-permute-start | bytes 245768 | tf_op jit(solution)/shard_map/ppermute | solution.py:96
  11.0 7.8 %collective-permute-start.2 = (bf16[8,32,128]{2,0,1:T(8,128)(2,1)S(1)}, bf16[8,32,128]{2,0,1:T(8,128)(2,1)S(1)}, u32[]{:S(2)}, u32[]{:S(2)}) collective-permute-start(bf16[8,32,128]{2,0,1:T(8,128)(2,1)S(1)} %get-tuple-element.39), channel_id=1, source_target_pairs={{0,4},{1,5},{2,6},{3,7},{4,0},{5,1},{6,2},{7,3},{8,12},{9,13},{10,... | collective-permute-start | bytes 196616 | tf_op jit(solution)/shard_map/ppermute | solution.py:97
  12.2 7.5 %collective-permute-start.3 = (bf16[8,32,128]{2,0,1:T(8,128)(2,1)S(1)}, bf16[8,32,128]{2,0,1:T(8,128)(2,1)S(1)}, u32[]{:S(2)}, u32[]{:S(2)}) collective-permute-start(bf16[8,32,128]{2,0,1:T(8,128)(2,1)S(1)} %get-tuple-element.40), channel_id=1, source_target_pairs={{4,32},{5,33},{6,34},{7,35},{12,40},{13,41},{14,42},{15,43},{20,48... | collective-permute-start | bytes 196616 | tf_op jit(solution)/shard_map/ppermute | solution.py:96
  18.4 15.3 %slice-start = ((s8[10354688]{0:T(1024)(128)(4,1)}), s8[4194304]{0:T(1024)(128)(4,1)S(1)}, s32[]{:S(2)}) async-start(s8[10354688]{0:T(1024)(128)(4,1)} %bitcast.114), calls=%async_computation | async-start | bytes 8388608
  19.9 11.8 %collective-permute-start.4 = (bf16[8,84,128]{2,0,1:T(8,128)(2,1)S(1)}, bf16[8,84,128]{2,0,1:T(8,128)(2,1)S(1)}, u32[]{:S(2)}, u32[]{:S(2)}) collective-permute-start(bf16[8,84,128]{2,0,1:T(8,128)(2,1)S(1)} %get-tuple-element.28), channel_id=1, source_target_pairs={{0,2},{1,3},{2,0},{3,1},{4,6},{5,7},{6,4},{7,5},{8,10},{9,11},{10,... | collective-permute-start | bytes 516104 | tf_op jit(solution)/shard_map/ppermute | solution.py:352
  20.0 28.9 %collective-permute-start.5 = (bf16[8,84,128]{2,0,1:T(8,128)(2,1)S(1)}, bf16[8,84,128]{2,0,1:T(8,128)(2,1)S(1)}, u32[]{:S(2)}, u32[]{:S(2)}) collective-permute-start(bf16[8,84,128]{2,0,1:T(8,128)(2,1)S(1)} %get-tuple-element.27), channel_id=1, source_target_pairs={{2,16},{3,17},{6,20},{7,21},{10,24},{11,25},{14,28},{15,29},{16,2}... | collective-permute-start | bytes 516104 | tf_op jit(solution)/shard_map/ppermute | solution.py:355
  31.9 2.2 %slice-start.1 = ((s8[10354688]{0:T(1024)(128)(4,1)}), s8[4194304]{0:T(1024)(128)(4,1)S(1)}, s32[]{:S(2)}) async-start(s8[10354688]{0:T(1024)(128)(4,1)} %bitcast.114), calls=%async_computation.1 | async-start | bytes 8388608
  32.7 2.2 %slice-start.2 = ((s8[10354688]{0:T(1024)(128)(4,1)}), s8[1966080]{0:T(1024)(128)(4,1)S(1)}, s32[]{:S(2)}) async-start(s8[10354688]{0:T(1024)(128)(4,1)} %bitcast.114), calls=%async_computation.2 | async-start | bytes 3932160
  48.9 1.0 %copy-start = (bf16[8,128,128]{2,1,0:T(8,128)(2,1)S(1)}, bf16[8,128,128]{2,1,0:T(8,128)(2,1)}, u32[]{:S(2)}) copy-start(bf16[8,128,128]{2,1,0:T(8,128)(2,1)} %shift.1) | copy-start | bytes 786436
  48.9 0.9 %copy-start.1 = (bf16[128,128]{1,0:T(8,128)(2,1)S(1)}, bf16[128,128]{1,0:T(8,128)(2,1)}, u32[]{:S(2)}) copy-start(bf16[128,128]{1,0:T(8,128)(2,1)} %constant.46.clone.perm) | copy-start | bytes 98308
  48.9 0.9 %copy-start.2 = (bf16[128,128]{1,0:T(8,128)(2,1)S(1)}, bf16[128,128]{1,0:T(8,128)(2,1)}, u32[]{:S(2)}) copy-start(bf16[128,128]{1,0:T(8,128)(2,1)} %constant.47.clone.fine_back) | copy-start | bytes 98308
  49.0 0.9 %copy-start.3 = (bf16[128,128]{1,0:T(8,128)(2,1)S(1)}, bf16[128,128]{1,0:T(8,128)(2,1)}, u32[]{:S(2)}) copy-start(bf16[128,128]{1,0:T(8,128)(2,1)} %constant.48.clone.parent_back) | copy-start | bytes 98308

commit v5 on v4

--- a/solution.py
+++ b/solution.py
@@ -169,11 +169,16 @@
     F = acc.shape[1] - xp.shape[1]
     rows = acc.shape[1]
 
-    def masked(place, column):
+    def spread_pair(one, two):
+        code = jnp.broadcast_to(one + 2.0 * two, (rows, 128)).astype(jnp.bfloat16)
+        high = jnp.clip(code - 1, 0, 1)
+        return code - 2 * high, high
+
+    def masked(place, spread):
         entry = table[place]
         row = pl.multiple_of((jnp.right_shift(entry, 9) & 511) * slab_rows, 16)
         value = jnp.concatenate([x[pl.ds(row, F), :], xp[jnp.right_shift(entry, 18)]], axis=0)
-        return value * jnp.broadcast_to(column, (rows, 128)).astype(jnp.bfloat16)
+        return value * spread
 
     longer = table[8 * slots]
 
@@ -184,9 +189,11 @@
             for at in range(0, count, CHUNK):
                 part = range(at, min(at + CHUNK, count))
                 place = octant * slots
-                left = jnp.concatenate(
-                    [masked(place + j, columns[:, first + j : first + j + 1]) for j in part], axis=1
-                )
+                spread = []
+                for j in range(part.start, part.stop, 2):
+                    at_j = first + j
+                    spread += spread_pair(columns[:, at_j : at_j + 1], columns[:, at_j + 1 : at_j + 2])
+                left = jnp.concatenate([masked(place + j, m) for j, m in zip(part, spread)], axis=1)
                 right = jnp.concatenate([kernels[table[place + j] & 511] for j in part], axis=0)
                 acc[octant] += jnp.dot(left, right, preferred_element_type=jnp.float32)
             return carry

time: 60.3 us -> 59.7 us (0.990)
    pallas_call x1, Pallas kernels: 14 us -> 13.4 us  [first_terms(): pl.pallas_call(kernel, out_shape=jax.ShapeDtypeStruct((8, rows, width), j...]
  transfers between devices with their start and end apart: 6 -> 6, of which waited for: 2 -> 2; matrix products, arithmetic and copies ran while one was open for 8% -> 9% of each run, Pallas kernels for 24% -> 23%
where the time goes in v5:
time: 59.7 us; the launch traced here: 59.4 us
  Pallas kernels  23.8 us (40%)
  starting transfers between devices  23.7 us (40%)
  local copies, waits for them, and re-layouts  6.54 us (11%)
  other arithmetic  2.59 us (4%)
  between operations  1.37 us (2%)
  waiting for transfers between devices  1.33 us (2%)
    pallas_call x1, Pallas kernels, first_terms(): pl.pallas_call(kernel, out_shape=jax.ShapeDtypeStruct((8, rows, width), j...  13.4 us
    ppermute x1, starting transfers between devices, on_device(): lax.ppermute(jnp.where(is_odd, top, bottom), 'box', pair_route(0, 1, fine...  11.6 us
    pallas_call x1, Pallas kernels, last_terms(): pl.pallas_call(kernel, out_shape=(jax.ShapeDtypeStruct((8 * F, width), jn...  10.1 us
    ppermute x2, starting transfers between devices, exchange(): lax.ppermute(odd_send, 'box', pair_route(dim, 1, low_bits, device_bits))  10.1 us
    unnamed x59, local copies, waits for them, and re-layouts  2.53 us
    select_n x3, other arithmetic, by_parity(): return jnp.where(is_odd, make(tables[1]), make(tables[0]))  2.11 us
    ppermute x2, starting transfers between devices, exchange(): lax.ppermute(even_send, 'box', pair_route(dim, 0, low_bits, device_bits))  1.97 us
    transpose x4, local copies, waits for them, and re-layouts, to_grid(): jnp.transpose(bitwise, tuple(axes_order) + extra)  1.84 us
  transfers between devices with their start and end apart: 6, of which 2 were waited for; matrix products, arithmetic and copies ran while one was open for 9% of the time, Pallas kernels for 23%

profile of v5, /device:TPU:31, one launch (start us, length us, event | category | flops | bytes accessed | tf_op | source)
XLA Modules:
  0.0 59.4 jit_solution(7716863067182120154)
XLA Ops:
  0.7 1.0 %copy.139 = bf16[2,2,2,2,2,2,2,8,128]{8,7,6,5,4,3,2,1,0:T(8,128)(2,1)S(1)} copy(bf16[2,2,2,2,2,2,2,8,128]{8,7,6,3,1,5,2,0,4:T(8,128)(2,1)} %bitcast.157) | data formatting | bytes 524288 | tf_op jit(solution)/shard_map/transpose | solution.py:41
  1.7 0.8 %copy.140 = bf16[2,2,2,2,8,128]{5,4,3,2,1,0:T(8,128)(2,1)S(1)} copy(bf16[2,2,2,2,8,128]{5,4,3,1,0,2:T(8,128)(2,1)} %bitcast.203) | data formatting | bytes 65536 | tf_op jit(solution)/shard_map/transpose | solution.py:41
  2.5 0.8 %collective-permute-start = (bf16[8,40,128]{2,0,1:T(8,128)(2,1)S(1)}, bf16[8,40,128]{2,0,1:T(8,128)(2,1)S(1)}, u32[]{:S(2)}, u32[]{:S(2)}) collective-permute-start(bf16[8,40,128]{2,0,1:T(8,128)(2,1)S(1)} %get-tuple-element.35), channel_id=1, source_target_pairs={{0,1},{1,0},{2,3},{3,2},{4,5},{5,4},{6,7},{7,6},{8,9},{9,8},{10,11... | collective-permute-start | bytes 245768 | tf_op jit(solution)/shard_map/ppermute | solution.py:97
  3.2 5.0 %collective-permute-start.1 = (bf16[8,40,128]{2,0,1:T(8,128)(2,1)S(1)}, bf16[8,40,128]{2,0,1:T(8,128)(2,1)S(1)}, u32[]{:S(2)}, u32[]{:S(2)}) collective-permute-start(bf16[8,40,128]{2,0,1:T(8,128)(2,1)S(1)} %get-tuple-element.36), channel_id=1, source_target_pairs={{1,8},{3,10},{5,12},{7,14},{8,1},{9,64},{10,3},{11,66},{12,5},{13,... | collective-permute-start | bytes 245768 | tf_op jit(solution)/shard_map/ppermute | solution.py:96
  8.2 0.7 %broadcast_select_fusion.12.table = s32[1009]{0:T(1024)S(1)} fusion(s32[1009]{0:T(1024)} %constant.38.clone, s32[1009]{0:T(1024)} %constant.39.clone, pred[]{:T(512)S(6)} %eq.9), kind=kLoop, calls=%fused_computation.94 | loop fusion | flops 1009 | bytes 12109 | tf_op jit(solution)/shard_map/jit(_where)/select_n | solution.py:322
  8.9 0.7 %broadcast_select_fusion.10 = (s32[8,256]{1,0:T(8,128)S(1)}, s32[8,256]{1,0:T(8,128)S(1)}) fusion(s32[8,256]{1,0:T(8,128)} %constant.44.clone, s32[8,256]{1,0:T(8,128)} %constant.45.clone, pred[]{:T(512)S(6)} %eq.9, s32[8,256]{1,0:T(8,128)} %constant.42.clone, s32[8,256]{1,0:T(8,128)} %constant.43.clone), kind=kLoop, calls=%fused_computation.92 | loop fusion | flops 4096 | bytes 49153 | tf_op jit(solution)/shard_map/jit(_where)/select_n | solution.py:322
  9.7 0.7 %broadcast_select_fusion.13.table = s32[577]{0:T(1024)S(1)} fusion(s32[577]{0:T(1024)} %constant.40.clone, s32[577]{0:T(1024)} %constant.41.clone, pred[]{:T(512)S(6)} %eq.9), kind=kLoop, calls=%fused_computation.95 | loop fusion | flops 577 | bytes 6925 | tf_op jit(solution)/shard_map/jit(_where)/select_n | solution.py:322
  10.3 0.4 collective-permute-done.1
  11.0 1.2 %collective-permute-start.2 = (bf16[8,32,128]{2,0,1:T(8,128)(2,1)S(1)}, bf16[8,32,128]{2,0,1:T(8,128)(2,1)S(1)}, u32[]{:S(2)}, u32[]{:S(2)}) collective-permute-start(bf16[8,32,128]{2,0,1:T(8,128)(2,1)S(1)} %get-tuple-element.39), channel_id=1, source_target_pairs={{0,4},{1,5},{2,6},{3,7},{4,0},{5,1},{6,2},{7,3},{8,12},{9,13},{10,... | collective-permute-start | bytes 196616 | tf_op jit(solution)/shard_map/ppermute | solution.py:97
  12.2 5.1 %collective-permute-start.3 = (bf16[8,32,128]{2,0,1:T(8,128)(2,1)S(1)}, bf16[8,32,128]{2,0,1:T(8,128)(2,1)S(1)}, u32[]{:S(2)}, u32[]{:S(2)}) collective-permute-start(bf16[8,32,128]{2,0,1:T(8,128)(2,1)S(1)} %get-tuple-element.40), channel_id=1, source_target_pairs={{4,32},{5,33},{6,34},{7,35},{12,40},{13,41},{14,42},{15,43},{20,48... | collective-permute-start | bytes 196616 | tf_op jit(solution)/shard_map/ppermute | solution.py:96
  17.3 0.2 copy.141
  17.6 0.2 copy.146
  17.9 0.1 copy.144
  18.0 0.1 copy.147
  18.2 0.2 copy.148.packed
  18.4 0.3 unpack.1.masks
  18.8 0.9 %collective-permute-done.3 = bf16[8,32,128]{2,0,1:T(8,128)(2,1)S(1)} collective-permute-done((bf16[8,32,128]{2,0,1:T(8,128)(2,1)S(1)}, bf16[8,32,128]{2,0,1:T(8,128)(2,1)S(1)}, u32[]{:S(2)}, u32[]{:S(2)}) %collective-permute-start.3) | collective-permute-done | bytes 65568 | tf_op jit(solution)/shard_map/ppermute | solution.py:96
  20.0 11.6 %collective-permute-start.5 = (bf16[8,84,128]{2,0,1:T(8,128)(2,1)S(1)}, bf16[8,84,128]{2,0,1:T(8,128)(2,1)S(1)}, u32[]{:S(2)}, u32[]{:S(2)}) collective-permute-start(bf16[8,84,128]{2,0,1:T(8,128)(2,1)S(1)} %get-tuple-element.27), channel_id=1, source_target_pairs={{2,16},{3,17},{6,20},{7,21},{10,24},{11,25},{14,28},{15,29},{16,2}... | collective-permute-start | bytes 516104 | tf_op jit(solution)/shard_map/ppermute | solution.py:362
  31.9 0.1 pad_maximum_fusion
  32.0 0.7 %fusion.6 = (bf16[8,6,4,8,128]{4,0,3,2,1:T(8,128)(2,1)S(1)}, bf16[8,6,4,8,128]{4,0,3,2,1:T(8,128)(2,1)S(1)}, bf16[8,6,4,8,128]{4,0,3,2,1:T(8,128)(2,1)S(1)}, bf1...) fusion(bf16[8,6,6,10,128]{4,0,3,2,1:T(8,128)(2,1)S(1)} %pad_max, ...), kind=kLoop, calls=%fused_computation.98 | loop fusion | bytes 7077888 | tf_op jit(solution)/shard_map/slice | solution.py:376
  33.0 0.1 copy_dynamic-update-slice_fusion.6
  33.1 0.1 copy_dynamic-update-slice_fusion.5
  33.2 0.1 copy_dynamic-update-slice_fusion.4
  33.3 0.1 copy_dynamic-update-slice_fusion.3
  33.4 0.1 copy_dynamic-update-slice_fusion.2
  33.5 0.1 copy_dynamic-update-slice_fusion.1
  33.6 0.1 copy_dynamic-update-slice_fusion
  33.8 0.3 slice-done.1
  34.1 0.8 %slice-done.2 = s8[1966080]{0:T(1024)(128)(4,1)S(1)} async-done(((s8[10354688]{0:T(1024)(128)(4,1)}), s8[1966080]{0:T(1024)(128)(4,1)S(1)}, s32[]{:S(2)}) %slice-start.2) | async-done | bytes 1966104
  34.9 13.4 %first_terms.1.sums = f32[8,144,128]{2,1,0:T(8,128)S(1)} custom-call(s32[1009]{0:T(1024)S(1)} %broadcast_select_fusion.12.table, f32[8,144,256]{2,1,0:T(8,128)S(1)} %unpack.1.masks, bf16[13824,128]{1,0:T(8,128)(2,1)S(1)} %bitcast.116, bf16[144,16,128]{2,1,0:T(8,128)(2,1)S(1)} %bitcast.119, bf16[316,128,128]{2,1,0:T(8,128)(2,1)S(1)} %bitcast.115), custom_call_target="tpu_custom_call" | custom-call | flops 4756340736 | bytes 3538944 | tf_op jit(solution)/shard_map/first_terms/pallas_call | solution.py:216
  49.1 0.1 copy-done
  49.2 10.1 %last_terms.1 = (bf16[1024,128]{1,0:T(8,128)(2,1)}, bf16[128,128]{1,0:T(8,128)(2,1)}) custom-call(s32[577]{0:T(1024)S(1)} %broadcast_select_fusion.13.table, f32[8,144,256]{2,1,0:T(8,128)S(1)} %unpack.1.masks, bf16[13824,128]{1,0:T(8,128)(2,1)S(1)} %bitcast.117, bf16[72,16,128]{2,1,0:T(8,128)(2,1)S(1)} %bitcast.118, bf16[316,128,128]{2,1,0:T(8,128)(2,1)S(1)} %bitcast.115, ...), custom_call_target="tpu_custom_call" | custom-call | tf_op jit(solution)/shard_map/last_terms/pallas_call | solution.py:257
  (97 shorter events, 1.7 us)
Async XLA Ops:
  0.6 16.7 %copy-start.4 = (s32[20,1024]{1,0:T(8,128)S(1)}, s32[20,1024]{1,0:T(8,128)}, u32[]{:S(2)}) copy-start(s32[20,1024]{1,0:T(8,128)} %param.19) | copy-start | bytes 245764
  0.6 17.2 %copy-start.5 = (s32[20,128]{1,0:T(8,128)S(1)}, s32[20,128]{1,0:T(8,128)}, u32[]{:S(2)}) copy-start(s32[20,128]{1,0:T(8,128)} %param.20) | copy-start | bytes 30724
  2.5 7.9 %collective-permute-start = (bf16[8,40,128]{2,0,1:T(8,128)(2,1)S(1)}, bf16[8,40,128]{2,0,1:T(8,128)(2,1)S(1)}, u32[]{:S(2)}, u32[]{:S(2)}) collective-permute-start(bf16[8,40,128]{2,0,1:T(8,128)(2,1)S(1)} %get-tuple-element.35), channel_id=1, source_target_pairs={{0,1},{1,0},{2,3},{3,2},{4,5},{5,4},{6,7},{7,6},{8,9},{9,8},{10,11... | collective-permute-start | bytes 245768 | tf_op jit(solution)/shard_map/ppermute | solution.py:97
  3.2 7.5 %collective-permute-start.1 = (bf16[8,40,128]{2,0,1:T(8,128)(2,1)S(1)}, bf16[8,40,128]{2,0,1:T(8,128)(2,1)S(1)}, u32[]{:S(2)}, u32[]{:S(2)}) collective-permute-start(bf16[8,40,128]{2,0,1:T(8,128)(2,1)S(1)} %get-tuple-element.36), channel_id=1, source_target_pairs={{1,8},{3,10},{5,12},{7,14},{8,1},{9,64},{10,3},{11,66},{12,5},{13,... | collective-permute-start | bytes 245768 | tf_op jit(solution)/shard_map/ppermute | solution.py:96
  11.0 7.8 %collective-permute-start.2 = (bf16[8,32,128]{2,0,1:T(8,128)(2,1)S(1)}, bf16[8,32,128]{2,0,1:T(8,128)(2,1)S(1)}, u32[]{:S(2)}, u32[]{:S(2)}) collective-permute-start(bf16[8,32,128]{2,0,1:T(8,128)(2,1)S(1)} %get-tuple-element.39), channel_id=1, source_target_pairs={{0,4},{1,5},{2,6},{3,7},{4,0},{5,1},{6,2},{7,3},{8,12},{9,13},{10,... | collective-permute-start | bytes 196616 | tf_op jit(solution)/shard_map/ppermute | solution.py:97
  12.2 7.5 %collective-permute-start.3 = (bf16[8,32,128]{2,0,1:T(8,128)(2,1)S(1)}, bf16[8,32,128]{2,0,1:T(8,128)(2,1)S(1)}, u32[]{:S(2)}, u32[]{:S(2)}) collective-permute-start(bf16[8,32,128]{2,0,1:T(8,128)(2,1)S(1)} %get-tuple-element.40), channel_id=1, source_target_pairs={{4,32},{5,33},{6,34},{7,35},{12,40},{13,41},{14,42},{15,43},{20,48... | collective-permute-start | bytes 196616 | tf_op jit(solution)/shard_map/ppermute | solution.py:96
  18.4 15.3 %slice-start = ((s8[10354688]{0:T(1024)(128)(4,1)}), s8[4194304]{0:T(1024)(128)(4,1)S(1)}, s32[]{:S(2)}) async-start(s8[10354688]{0:T(1024)(128)(4,1)} %bitcast.114), calls=%async_computation | async-start | bytes 8388608
  19.9 11.8 %collective-permute-start.4 = (bf16[8,84,128]{2,0,1:T(8,128)(2,1)S(1)}, bf16[8,84,128]{2,0,1:T(8,128)(2,1)S(1)}, u32[]{:S(2)}, u32[]{:S(2)}) collective-permute-start(bf16[8,84,128]{2,0,1:T(8,128)(2,1)S(1)} %get-tuple-element.28), channel_id=1, source_target_pairs={{0,2},{1,3},{2,0},{3,1},{4,6},{5,7},{6,4},{7,5},{8,10},{9,11},{10,... | collective-permute-start | bytes 516104 | tf_op jit(solution)/shard_map/ppermute | solution.py:359
  20.0 28.3 %collective-permute-start.5 = (bf16[8,84,128]{2,0,1:T(8,128)(2,1)S(1)}, bf16[8,84,128]{2,0,1:T(8,128)(2,1)S(1)}, u32[]{:S(2)}, u32[]{:S(2)}) collective-permute-start(bf16[8,84,128]{2,0,1:T(8,128)(2,1)S(1)} %get-tuple-element.27), channel_id=1, source_target_pairs={{2,16},{3,17},{6,20},{7,21},{10,24},{11,25},{14,28},{15,29},{16,2}... | collective-permute-start | bytes 516104 | tf_op jit(solution)/shard_map/ppermute | solution.py:362
  31.9 2.2 %slice-start.1 = ((s8[10354688]{0:T(1024)(128)(4,1)}), s8[4194304]{0:T(1024)(128)(4,1)S(1)}, s32[]{:S(2)}) async-start(s8[10354688]{0:T(1024)(128)(4,1)} %bitcast.114), calls=%async_computation.1 | async-start | bytes 8388608
  32.7 2.2 %slice-start.2 = ((s8[10354688]{0:T(1024)(128)(4,1)}), s8[1966080]{0:T(1024)(128)(4,1)S(1)}, s32[]{:S(2)}) async-start(s8[10354688]{0:T(1024)(128)(4,1)} %bitcast.114), calls=%async_computation.2 | async-start | bytes 3932160
  48.3 1.0 %copy-start = (bf16[8,128,128]{2,1,0:T(8,128)(2,1)S(1)}, bf16[8,128,128]{2,1,0:T(8,128)(2,1)}, u32[]{:S(2)}) copy-start(bf16[8,128,128]{2,1,0:T(8,128)(2,1)} %shift.1) | copy-start | bytes 786436
  48.3 0.9 %copy-start.1 = (bf16[128,128]{1,0:T(8,128)(2,1)S(1)}, bf16[128,128]{1,0:T(8,128)(2,1)}, u32[]{:S(2)}) copy-start(bf16[128,128]{1,0:T(8,128)(2,1)} %constant.46.clone.perm) | copy-start | bytes 98308
  48.3 0.9 %copy-start.2 = (bf16[128,128]{1,0:T(8,128)(2,1)S(1)}, bf16[128,128]{1,0:T(8,128)(2,1)}, u32[]{:S(2)}) copy-start(bf16[128,128]{1,0:T(8,128)(2,1)} %constant.47.clone.fine_back) | copy-start | bytes 98308
  48.3 0.9 %copy-start.3 = (bf16[128,128]{1,0:T(8,128)(2,1)S(1)}, bf16[128,128]{1,0:T(8,128)(2,1)}, u32[]{:S(2)}) copy-start(bf16[128,128]{1,0:T(8,128)(2,1)} %constant.48.clone.parent_back) | copy-start | bytes 98308
